TPU v7x, 256 devices: a whole 4x4x8 slice. The times are simulated.
256 devices in a mesh: group: 16 (over z_hi, x, core), dp: 16 (over z_lo, y).
Axes of the slice: x: 4, y: 4, z: 8 (z_hi: 2, z_lo: 4; z = z_hi * 4 + z_lo), core: 2. Of those that a mesh axis runs over, the one named last changes fastest.
Arguments:
- query_hidden: bfloat16 [2048, 32, 768], P(('dp', 'group')), may hold values from -6 to 6
- passage_hidden: bfloat16 [4096, 128, 768], P(('dp', 'group')), may hold values from -6 to 6
- projection: bfloat16 [768, 128], replicated, may hold values from -0.21875 to 0.21875
- positive: int32 [2048], P(('dp', 'group')), may hold values from 0 to 255
- hard_ids: int32 [2048, 32], P(('dp', 'group')), may hold values from -1 to 255, as said below
- passage_len: int32 [4096], P(('dp', 'group')), may hold values from 16 to 128, as said below
Outputs:
- losses: float32 [2048], P(('dp', 'group'))
- grad_proj: float32 [768, 128], replicated
- grad_query: bfloat16 [2048, 32, 768], P(('dp', 'group'))
- grad_passage: bfloat16 [4096, 128, 768], P(('dp', 'group'))
Inputs may be any that keep to these rules, and one draw needn't show every extreme that they name: A passage's first passage_len tokens are live, the rest padding. `hard_ids`: A query's filled slots come first, from 8 to 32 of them; the rest hold -1. Slots may repeat a passage or name the positive.
All inputs are finite; a program needn't handle non-finite values.
Results may differ from a plain program's by a relative error of at most 0.017.
Values may be sent and summed in bfloat16 or wider, within the bound.
A program may use at most 64 MiB of HBM per device.

v0:
```python
import jax
import jax.numpy as jnp
from jax import lax
from jax.sharding import Mesh
from jax.sharding import PartitionSpec as P

GROUP_DP = ("group_0", "group_1", "group_2", "dp_0", "dp_1")
GROUP = ("group_0", "group_1", "group_2")
DP = ("dp_0", "dp_1")
DP_GROUP = ("dp_0", "dp_1", "group_0", "group_1", "group_2")


smooth_temp = 0.1
norm_eps = 1e-06


def one_axis_at_a_time(array, axes):
    for axis in axes:
        array = lax.psum(array, axis)
    return array


def copy_for_each(array, axis):
    copies = jnp.broadcast_to(array, (lax.axis_size(axis), *array.shape))
    return lax.all_to_all(copies, axis, split_axis=0, concat_axis=0, tiled=True)


def laid_out(tiles, dim):
    shape = list(tiles.shape[1:])
    shape[dim] *= tiles.shape[0]
    return jnp.moveaxis(tiles, 0, dim).reshape(shape)


def gather_directly(array, axis, dim):
    tiles = copy_for_each(array, axis)
    return laid_out(tiles, dim)


def cut_along(array, dim, devices):
    shape = array.shape
    tiles = array.reshape(*shape[:dim], devices, shape[dim] // devices, *shape[dim + 1 :])
    return jnp.moveaxis(tiles, dim, 0)


def turned_blocks(tiles, axes, order):
    shape = [lax.axis_size(a) for a in axes]
    tiles = tiles.reshape(*shape, *tiles.shape[1:])
    for k in order:
        tiles = lax.all_to_all(tiles, axes[k], split_axis=k, concat_axis=k, tiled=True)
    return tiles.reshape(-1, *tiles.shape[len(axes) :])


def core_and_chips(array, groups, order, split_dim, concat_dim):
    devices = lax.axis_size(groups[0]) * lax.axis_size(groups[1])
    tiles = cut_along(array, split_dim, devices)
    return laid_out(turned_blocks(tiles, groups, order), concat_dim)


def summed_on_arrival(array, axis, dim):
    devices = lax.axis_size(axis)
    tiles = lax.all_to_all(cut_along(array, dim, devices), axis, 0, 0, tiled=True)
    return jnp.sum(tiles.astype(jnp.float32), axis=0)


def normalize(projected):
    return projected * lax.rsqrt(jnp.sum(projected * projected, axis=-1, keepdims=True) + norm_eps)


def contract_last(left, right):
    return lax.dot_general(
        left, right, (((1,), (1,)), ((), ())), preferred_element_type=jnp.float32
    )


def contract_first(left, right):
    return lax.dot_general(
        left, right, (((0,), (0,)), ((), ())), preferred_element_type=jnp.float32
    )


def smooth_scores(query_rows, passage_rows, usable):
    similar = contract_last(query_rows, passage_rows)
    similar = similar.reshape(similar.shape[0], usable.shape[0], usable.shape[1])
    summed = jnp.sum(jnp.where(usable[None], jnp.exp(similar / smooth_temp), 0.0), axis=-1)
    return smooth_temp * jnp.log(summed)


def token_grads(query_rows, passage_rows, usable, smooth, weights):
    similar = contract_last(query_rows, passage_rows)
    similar = similar.reshape(similar.shape[0], usable.shape[0], usable.shape[1])
    shares = jnp.where(
        usable[None], jnp.exp(similar / smooth_temp - smooth[:, :, None] / smooth_temp), 0.0
    )
    coefficient = (weights[:, :, None] * shares).astype(jnp.bfloat16)
    coefficient = coefficient.reshape(query_rows.shape[0], passage_rows.shape[0])
    query_part = jnp.dot(coefficient, passage_rows, preferred_element_type=jnp.float32)
    passage_part = contract_first(coefficient, query_rows)
    return (query_part, passage_part)


def hard_counts(hard_ids, pool_size):
    columns = jnp.arange(pool_size, dtype=jnp.int32)
    return jnp.sum((hard_ids[:, :, None] == columns[None, None, :]).astype(jnp.float32), axis=1)


def finish_loss(scores, positive, hard_ids, total_slots):
    counts = hard_counts(hard_ids, scores.shape[1])
    boost = scores.shape[1] / hard_ids.shape[1]
    hard_total = one_axis_at_a_time(jnp.sum(counts * jnp.exp(scores)), GROUP_DP)
    hard_mean = hard_total / total_slots
    columns = jnp.arange(scores.shape[1], dtype=jnp.int32)
    chosen = positive[:, None] == columns[None, :]
    pos_score = jnp.sum(jnp.where(chosen, scores, 0.0), axis=1, keepdims=True)
    reweight = 1.0 + jnp.where(chosen, 0.0, boost * counts * jnp.exp(scores - jnp.log(hard_mean)))
    weighted = reweight * jnp.exp(scores - pos_score)
    partition = jnp.sum(weighted, axis=1, keepdims=True)
    losses = jnp.log(partition[:, 0])
    score_grad = weighted / partition - chosen.astype(jnp.float32)
    return (losses, score_grad)


def local(query_hidden, passage_hidden, projection, positive, hard_ids, passage_len):
    query_count = query_hidden.shape[0]
    query_len = query_hidden.shape[1]
    hidden_width = query_hidden.shape[2]
    passage_count = passage_hidden.shape[0]
    passage_tokens = passage_hidden.shape[1]
    embed_width = projection.shape[1]
    groups = lax.axis_size(GROUP)
    total_slots = query_count * groups * lax.axis_size(DP) * hard_ids.shape[1]
    block_rows = query_count * query_len
    query_flat = query_hidden.reshape(block_rows, hidden_width)
    passage_flat = passage_hidden.reshape(passage_count * passage_tokens, hidden_width)
    query_pre = jnp.dot(query_flat, projection, preferred_element_type=jnp.float32)
    passage_pre = jnp.dot(passage_flat, projection, preferred_element_type=jnp.float32)
    query_embed = normalize(query_pre).astype(jnp.bfloat16)
    passage_embed = normalize(passage_pre).astype(jnp.bfloat16)
    token_index = jnp.arange(passage_tokens, dtype=jnp.int32)
    gathered = gather_directly(query_embed, GROUP, 0)
    query_blocks = gathered.reshape(groups, block_rows, embed_width)
    usable = token_index[None, :] < passage_len[:, None]
    smooth_blocks = lax.map(
        lambda query_block: smooth_scores(query_block, passage_embed, usable), query_blocks
    )
    local_scores = jnp.sum(
        smooth_blocks.reshape(groups * query_count, query_len, passage_count), axis=1
    )
    scores = lax.all_to_all(local_scores, GROUP, split_axis=0, concat_axis=1, tiled=True)
    losses, score_grad = finish_loss(scores, positive, hard_ids, total_slots)
    returned = core_and_chips(score_grad, (("group_0", "group_1"), "group_2"), (1, 0), 1, 0)
    weight_blocks = jnp.repeat(returned, query_len, axis=0).reshape(
        groups, block_rows, passage_count
    )

    def backward_block(running, members):
        query_part, passage_part = token_grads(
            members[0], passage_embed, usable, members[1], members[2]
        )
        rounded = lax.optimization_barrier(passage_part.astype(jnp.bfloat16))
        return (running + rounded.astype(jnp.float32), query_part)

    initial = jnp.zeros((passage_count * passage_tokens, embed_width), jnp.float32)
    passage_grad, query_parts = lax.scan(
        backward_block, initial, (query_blocks, smooth_blocks, weight_blocks)
    )
    query_grad = summed_on_arrival(
        query_parts.reshape(groups * block_rows, embed_width).astype(jnp.bfloat16), GROUP, 0
    )
    query_back = jax.vjp(normalize, query_pre)[1](query_grad)[0].astype(jnp.bfloat16)
    passage_back = jax.vjp(normalize, passage_pre)[1](passage_grad)[0].astype(jnp.bfloat16)
    grad_query = (
        contract_last(query_back, projection)
        .astype(jnp.bfloat16)
        .reshape(query_count, query_len, hidden_width)
    )
    grad_passage = (
        contract_last(passage_back, projection)
        .astype(jnp.bfloat16)
        .reshape(passage_count, passage_tokens, hidden_width)
    )
    local_weight = contract_first(query_flat, query_back) + contract_first(
        passage_flat, passage_back
    )
    grad_proj = lax.psum(local_weight, GROUP_DP)
    return (losses, grad_proj, grad_query, grad_passage)


def solution(mesh):
    split = Mesh(
        mesh.devices.reshape(2, 4, 2, 4, 4), ("group_0", "group_1", "group_2", "dp_0", "dp_1")
    )
    placed = (
        P(DP_GROUP, None, None),
        P(DP_GROUP, None, None),
        P(),
        P(DP_GROUP),
        P(DP_GROUP, None),
        P(DP_GROUP),
    )
    return jax.shard_map(
        local,
        mesh=split,
        in_specs=placed,
        out_specs=(P(DP_GROUP), P(), P(DP_GROUP, None, None), P(DP_GROUP, None, None)),
        check_vma=False,
    )
```

profile of v0, /device:TPU:1, one launch (start us, length us, event | category | flops | bytes accessed | tf_op | source)
XLA Modules:
  0.0 654.9 jit_solution(4493918222659081789)
XLA Ops:
  12.1 12.4 %all-to-all-start = ((bf16[16,256,128]{2,1,0:T(8,128)(2,1)}), bf16[16,256,128]{2,1,0:T(8,128)(2,1)}, u32[]{:S(2)}, u32[]{:S(2)}) async-start(bf16[16,256,128]{2,1,0:T(8,128)(2,1)} %broadcast_in_dim.71), calls=%async_computation | async-start | bytes 2097152 | tf_op jit(solution)/shard_map/all_to_all | solution.py:25
  30.4 16.1 %all-to-all-done = bf16[16,256,128]{2,1,0:T(8,128)(2,1)} async-done(((bf16[16,256,128]{2,1,0:T(8,128)(2,1)}), bf16[16,256,128]{2,1,0:T(8,128)(2,1)}, u32[]{:S(2)}, u32[]{:S(2)}) %all-to-all-start) | async-done | bytes 1048608 | tf_op jit(solution)/shard_map/all_to_all | solution.py:25
  46.5 38.2 %while.24 = (s32[]{:T(128)}, f32[16,256,16]{1,2,0:T(8,128)}, bf16[16,256,128]{2,1,0:T(8,128)(2,1)}, bf16[2048,128]{1,0:T(8,128)(2,1)}, s32[16]{0:T(128)S(1)}, /*index=5*/s32[]{:T(128)}) while((s32[]{:T(128)}, f32[16,256,16]{1,2,0:T(8,128)}, bf16[16,256,128]{2,1,0:T(8,128)(2,1)}, bf16[2048,128]{1,0:T(8,128)(2,1)}, s32[16]{0:T(128)S(1)}, ...), condition=%wide.region_5.6_spmd.clone, body=%wide.region_3.0_spmd.clone.sunk | while | flops 135792640 | bytes 644229 | solution.py:142
  91.0 10.3 %all-to-all-start.1 = ((f32[16,1,128]{2,1,0:T(1,128)}), f32[16,1,128]{2,1,0:T(1,128)}, u32[]{:S(2)}, u32[]{:S(2)}) async-start(f32[16,1,128]{2,1,0:T(1,128)} %reshape.151), calls=%async_computation.1 | async-start | bytes 16384 | tf_op jit(solution)/shard_map/all_to_all | solution.py:148
  102.1 8.5 %all-to-all-done.1 = f32[16,1,128]{2,1,0:T(1,128)} async-done(((f32[16,1,128]{2,1,0:T(1,128)}), f32[16,1,128]{2,1,0:T(1,128)}, u32[]{:S(2)}, u32[]{:S(2)}) %all-to-all-start.1) | async-done | bytes 8224 | tf_op jit(solution)/shard_map/all_to_all | solution.py:148
  116.1 8.3 %psum.42 = f32[]{:T(128)} all-reduce(f32[]{:T(128)} %get-tuple-element.222), channel_id=1, replica_groups=mesh['group_0'=2,'group_1'=4,'group_2'=2,'dp_0'=4,'dp_1'=4] {'group_0'}, use_global_device_ids=true, to_apply=%region_8.9 | all-reduce | flops 1 | bytes 8 | tf_op jit(solution)/shard_map/psum | solution.py:19
  124.4 7.5 %psum.43 = f32[]{:T(128)} all-reduce(f32[]{:T(128)} %psum.42), channel_id=1, replica_groups=mesh['group_0'=2,'group_1'=4,'group_2'=2,'dp_0'=4,'dp_1'=4] {'group_1'}, use_global_device_ids=true, to_apply=%region_9.10 | all-reduce | flops 1 | bytes 8 | tf_op jit(solution)/shard_map/psum | solution.py:19
  131.9 6.7 %psum.44 = f32[]{:T(128)} all-reduce(f32[]{:T(128)} %psum.43), channel_id=1, replica_groups=mesh['group_0'=2,'group_1'=4,'group_2'=2,'dp_0'=4,'dp_1'=4] {'group_2'}, use_global_device_ids=true, to_apply=%region_10.11 | all-reduce | flops 1 | bytes 8 | tf_op jit(solution)/shard_map/psum | solution.py:19
  138.7 11.3 %psum.45 = f32[]{:T(128)} all-reduce(f32[]{:T(128)} %psum.44), channel_id=1, replica_groups=mesh['group_0'=2,'group_1'=4,'group_2'=2,'dp_0'=4,'dp_1'=4] {'dp_0'}, use_global_device_ids=true, to_apply=%region_11.12 | all-reduce | flops 1 | bytes 8 | tf_op jit(solution)/shard_map/psum | solution.py:19
  150.0 9.3 %psum.46 = f32[]{:T(128)} all-reduce(f32[]{:T(128)} %psum.45), channel_id=1, replica_groups=mesh['group_0'=2,'group_1'=4,'group_2'=2,'dp_0'=4,'dp_1'=4] {'dp_1'}, use_global_device_ids=true, to_apply=%region_12.13 | all-reduce | flops 1 | bytes 8 | tf_op jit(solution)/shard_map/psum | solution.py:19
  162.6 8.6 %all_to_all.36 = f32[2,1,1024]{2,1,0:T(1,128)S(1)} all-to-all(f32[2,1,1024]{2,1,0:T(1,128)} %reshape.153), channel_id=1, replica_groups=mesh['group_0'=2,'group_1'=4,'group_2'=2,'dp_0'=4,'dp_1'=4] {'group_2'}, dimensions={0} | all-to-all | bytes 16384 | tf_op jit(solution)/shard_map/all_to_all | solution.py:49
  175.4 3.3 all-to-all-start.3
  178.8 8.9 %all-to-all-done.3 = f32[8,1,256]{2,1,0:T(1,128)S(1)} async-done(((f32[8,1,256]{2,1,0:T(1,128)}), f32[8,1,256]{2,1,0:T(1,128)S(1)}, u32[]{:S(2)}, u32[]{:S(2)}) %all-to-all-start.3) | async-done | bytes 8224 | tf_op jit(solution)/shard_map/all_to_all | solution.py:49
  194.6 162.9 %while.25 = (s32[]{:T(128)}, f32[2048,128]{1,0:T(8,128)}, bf16[16,256,128]{2,1,0:T(8,128)(2,1)}, f32[16,256,16]{1,0,2:T(8,128)}, bf16[16,256,128]{2,1,0:T(8,128)...) while((s32[]{:T(128)}, f32[2048,128]{1,0:T(8,128)}, ...), condition=%wide.region_16.17_spmd.clone, body=%wide.region_15.16_spmd.clone.sunk | while | flops 406329344 | bytes 18224908 | solution.py:163
  211.0 2.5 select_add_fusion.2
  221.2 2.5 select_add_fusion.2
  231.4 2.5 select_add_fusion.2
  241.6 2.5 select_add_fusion.2
  251.8 2.5 select_add_fusion.2
  262.0 2.5 select_add_fusion.2
  272.2 2.5 select_add_fusion.2
  282.5 2.5 select_add_fusion.2
  292.6 2.5 select_add_fusion.2
  302.8 2.5 select_add_fusion.2
  313.0 2.5 select_add_fusion.2
  323.3 2.5 select_add_fusion.2
  333.5 2.5 select_add_fusion.2
  357.5 5.7 all-to-all-start.4
  363.8 2.6 copy.78
  368.7 2.7 convolution_convert_fusion.1
  372.7 18.9 %all-to-all-done.4 = bf16[16,256,128]{2,1,0:T(8,128)(2,1)} async-done(((bf16[16,256,128]{2,1,0:T(8,128)(2,1)}), bf16[16,256,128]{2,1,0:T(8,128)(2,1)}, u32[]{:S(2)}, u32[]{:S(2)}) %all-to-all-start.4) | async-done | bytes 1048608 | tf_op jit(solution)/shard_map/all_to_all | solution.py:61
  400.3 245.8 %all-reduce.2.cloned.1.call-done = f32[768,128]{0,1:T(8,128)} async-done(((f32[768,128]{0,1:T(8,128)}), f32[768,128]{0,1:T(8,128)}) %all-reduce.2.cloned.1.call-update) | async-done | bytes 393232 | tf_op jit(solution)/shard_map/psum | solution.py:184
  (327 shorter events, 219.3 us)
Async XLA Ops:
  7.2 17.4 %copy-start = (bf16[16,128,768]{2,1,0:T(8,128)(2,1)S(1)}, bf16[16,128,768]{2,1,0:T(8,128)(2,1)}, u32[]{:S(2)}) copy-start(bf16[16,128,768]{2,1,0:T(8,128)(2,1)} %param.11) | copy-start | bytes 9437188
  7.2 17.4 %copy-start.7 = (bf16[768,128]{1,0:T(8,128)(2,1)S(1)}, bf16[768,128]{1,0:T(8,128)(2,1)}, u32[]{:S(2)}) copy-start(bf16[768,128]{1,0:T(8,128)(2,1)} %param.12) | copy-start | bytes 589828
  12.1 34.4 %all-to-all-start = ((bf16[16,256,128]{2,1,0:T(8,128)(2,1)}), bf16[16,256,128]{2,1,0:T(8,128)(2,1)}, u32[]{:S(2)}, u32[]{:S(2)}) async-start(bf16[16,256,128]{2,1,0:T(8,128)(2,1)} %broadcast_in_dim.71), calls=%async_computation | async-start | bytes 2097152 | tf_op jit(solution)/shard_map/all_to_all | solution.py:25
  25.7 20.7 %copy-start.8 = (f32[2048]{0:T(1024)}, f32[2048]{0:T(1024)S(1)}, u32[]{:S(2)}) copy-start(f32[2048]{0:T(1024)S(1)} %get-tuple-element.256) | copy-start | bytes 24580
  25.7 3.9 copy-start.16
  25.8 20.7 %copy-start.10 = (s32[16]{0:T(128)S(1)}, s32[16]{0:T(128)}, u32[]{:S(2)}) copy-start(s32[16]{0:T(128)} %param.15) | copy-start | bytes 196
  91.0 19.6 %all-to-all-start.1 = ((f32[16,1,128]{2,1,0:T(1,128)}), f32[16,1,128]{2,1,0:T(1,128)}, u32[]{:S(2)}, u32[]{:S(2)}) async-start(f32[16,1,128]{2,1,0:T(1,128)} %reshape.151), calls=%async_computation.1 | async-start | bytes 16384 | tf_op jit(solution)/shard_map/all_to_all | solution.py:148
  161.8 32.8 %copy-start.11 = (s32[16]{0:T(128)S(1)}, s32[16]{0:T(128)}, u32[]{:S(2)}) copy-start(s32[16]{0:T(128)} %param.15) | copy-start | bytes 196
  175.4 12.2 %all-to-all-start.3 = ((f32[8,1,256]{2,1,0:T(1,128)}), f32[8,1,256]{2,1,0:T(1,128)S(1)}, u32[]{:S(2)}, u32[]{:S(2)}) async-start(f32[8,1,256]{2,1,0:T(1,128)} %reshape.155), calls=%async_computation.3 | async-start | bytes 16384 | tf_op jit(solution)/shard_map/all_to_all | solution.py:49
  211.0 2.6 copy-start.2
  211.0 2.6 copy-start.3
  221.2 2.6 copy-start.2
  221.2 2.6 copy-start.3
  231.4 2.6 copy-start.3
  241.6 2.6 copy-start.3
  251.8 2.6 copy-start.3
  262.0 2.6 copy-start.3
  272.2 2.6 copy-start.3
  282.5 2.6 copy-start.3
  292.6 2.6 copy-start.3
  302.8 2.6 copy-start.3
  313.0 2.6 copy-start.3
  323.3 2.6 copy-start.3
  333.5 2.6 copy-start.3
  343.7 2.6 copy-start.3
  353.9 2.6 copy-start.3
  357.5 5.7 copy-start.18
  357.5 34.1 %all-to-all-start.4 = ((bf16[16,256,128]{2,1,0:T(8,128)(2,1)}), bf16[16,256,128]{2,1,0:T(8,128)(2,1)}, u32[]{:S(2)}, u32[]{:S(2)}) async-start(bf16[16,256,128]{2,1,0:T(8,128)(2,1)} %get-tuple-element.75), calls=%async_computation.4 | async-start | bytes 2097152 | tf_op jit(solution)/shard_map/all_to_all | solution.py:61
  363.2 282.9 %all-reduce.2.cloned.1.call-start = ((), (), s32[]{:S(2)}) async-start(), calls=%async_computation.5 | async-start | bytes 786432 | tf_op jit(solution)/shard_map/psum | solution.py:184
  363.8 4.4 copy-start.9
  371.4 24.8 %copy-start.15 = (f32[256]{0:T(256)S(1)}, f32[256]{0:T(256)}, u32[]{:S(2)}) copy-start(f32[256]{0:T(256)} %copy-done.14) | copy-start | bytes 3076
  371.4 24.9 %copy-start.13 = (f32[256]{0:T(256)S(1)}, f32[256]{0:T(256)}, u32[]{:S(2)}) copy-start(f32[256]{0:T(256)} %copy-done.12) | copy-start | bytes 3076
  (37 other events, 60.4 us)
Sparse Core Ops, SparseCore 0:
  399.4 246.6 all-reduce.1
where the time goes:
time: 659 us; the launch traced here: 655 us
  waiting for transfers between devices  298 us (45%)
  matrix products  116 us (18%)
  other arithmetic  82.1 us (12%)
  local copies, waits for them, and re-layouts  59.9 us (9%)
  blocking collectives  51.8 us (8%)
  starting transfers between devices  31.7 us (5%)
  between operations  15 us (2%)
    psum x1, waiting for transfers between devices, local(): grad_proj = lax.psum(local_weight, GROUP_DP)  246 us
    dot_general x34, matrix products, contract_last(): lax.dot_general(left, right, (((1,), (1,)), ((), ())), preferred_element_...  58.5 us
    psum x5, blocking collectives, one_axis_at_a_time(): array = lax.psum(array, axis)  43.2 us
    add x16, other arithmetic, backward_block(): return (running + rounded.astype(jnp.float32), query_part)  40.5 us
    dot_general x18, matrix products, contract_first(): lax.dot_general(left, right, (((0,), (0,)), ((), ())), preferred_element_...  36.8 us
    all_to_all x1, waiting for transfers between devices, summed_on_arrival(): lax.all_to_all(cut_along(array, dim, devices), axis, 0, 0, tiled=True)  18.9 us
    dot_general x16, matrix products, token_grads(): jnp.dot(coefficient, passage_rows, preferred_element_type=jnp.float32)  17.6 us
    all_to_all x1, waiting for transfers between devices, copy_for_each(): return lax.all_to_all(copies, axis, split_axis=0, concat_axis=0, tiled=True)  16.1 us
  transfers between devices with their start and end apart: 5, of which 5 were waited for; matrix products, arithmetic and copies ran while one was open for 2% of the time, Pallas kernels for 0%

commit v1 on v0

v1 whole, which is shorter than its diff:
```python
import functools

import jax
import jax.numpy as jnp
from jax import lax
from jax.experimental import pallas as pl
from jax.experimental.pallas import tpu as pltpu
from jax.sharding import Mesh
from jax.sharding import PartitionSpec as P

MESH = pl.DeviceIdType.MESH
F32 = jnp.float32
BF16 = jnp.bfloat16

AXES = ("zh", "x", "c", "zl", "y")
SPLIT = ("zl", "y", "zh", "x", "c")
norm_eps = 1e-06
EXP2_SCALE = 14.426950408889634
SHIFT = 12.0
HIGHEST = lax.Precision.HIGHEST

GROUP_RELATIVE = [(dz, dx, dc) for dz in range(2) for dx in range(4) for dc in range(2)]


def slot_of(dz, dx, dc):
    return dz * 8 + dx * 2 + dc


def back(d, n):
    return (n - d) % n


def contract_last(left, right):
    return lax.dot_general(
        left, right, (((1,), (1,)), ((), ())), preferred_element_type=F32
    )


def norm_vjp(pre, grad):
    scale = lax.rsqrt(jnp.sum(pre * pre, axis=-1, keepdims=True) + norm_eps)
    along = jnp.sum(pre * grad, axis=-1, keepdims=True)
    return scale * grad - pre * (scale * scale * scale * along)


class Sems:
    def __init__(self):
        self.total = 0

    def take(self, count):
        first = self.total
        self.total += count
        return first


SEND = Sems()
RECV = Sems()
LOCAL = Sems()
S_GATHER, R_GATHER = SEND.take(15), RECV.take(16)
S_META, R_META = SEND.take(16), RECV.take(16)
S_STATS, R_STATS = SEND.take(16), RECV.take(16)
S_HARD, R_HARD = SEND.take(16), RECV.take(16)
S_QC, R_QC = SEND.take(8), RECV.take(8)
S_QX, R_QX = SEND.take(8), RECV.take(8)
S_QZ, R_QZ = SEND.take(1), RECV.take(1)
S_AC, R_AC = SEND.take(1), RECV.take(1)
S_AX, R_AX = SEND.take(4), RECV.take(4)
S_AY, R_AY = SEND.take(4), RECV.take(4)
S_AZ, R_AZ = SEND.take(8), RECV.take(8)
S_GY, R_GY = SEND.take(4), RECV.take(4)
S_GX, R_GX = SEND.take(4), RECV.take(4)
S_GC, R_GC = SEND.take(1), RECV.take(1)
P_CHUNKS = 4
L_IN = LOCAL.take(P_CHUNKS)
L_OUT = LOCAL.take(P_CHUNKS)


def kernel(
    plen,
    positive,
    query_hidden,
    passage_hbm,
    projection,
    hard_ids,
    losses_out,
    proj_out,
    gq_out,
    gp_hbm,
    ph,
    q_pre,
    p_pre,
    pe,
    pe_t,
    qh_t,
    qg,
    e_ref,
    sums,
    w_ref,
    pg,
    meta,
    meta_rows,
    counts_ref,
    chosen_ref,
    score_ref,
    st_send,
    st_recv,
    h_send,
    h_recv,
    qgt,
    rc,
    cs,
    own_c,
    rx,
    zs,
    rz,
    pb_t,
    gp_buf,
    w_loc,
    ac_recv,
    h_core,
    ax_recv,
    h_x,
    ay_recv,
    h_y,
    az_recv,
    fin,
    ssem,
    rsem,
    lsem,
):
    zh, x, c = lax.axis_index("zh"), lax.axis_index("x"), lax.axis_index("c")
    zl, y = lax.axis_index("zl"), lax.axis_index("y")
    z = zh * 4 + zl

    def at_x(d):
        return {"x": lax.rem(x + d, 4)}

    def at_y(d):
        return {"y": lax.rem(y + d, 4)}

    def at_z(d):
        there = lax.rem(z + d, 8)
        return {"zh": there // 4, "zl": lax.rem(there, 4)}

    def in_group(dz, dx, dc):
        return {"zh": lax.rem(zh + dz, 2), "x": lax.rem(x + dx, 4), "c": lax.rem(c + dc, 2)}

    def in_dp(dl, dy):
        return {"zl": lax.rem(zl + dl, 4), "y": lax.rem(y + dy, 4)}

    partner = {"c": 1 - c}
    across = {"zh": 1 - zh}

    def group_of(dz, dx, dc):
        return (lax.rem(zh + dz, 2) * 4 + lax.rem(x + dx, 4)) * 2 + lax.rem(c + dc, 2)

    def push(src, dst, s, r, device):
        pltpu.make_async_remote_copy(
            src_ref=src,
            dst_ref=dst,
            send_sem=ssem.at[s],
            recv_sem=rsem.at[r],
            device_id=device,
            device_id_type=MESH,
        ).start()

    def arrived(dst, r):
        pltpu.make_async_remote_copy(
            src_ref=dst,
            dst_ref=dst,
            send_sem=ssem.at[0],
            recv_sem=rsem.at[r],
            device_id=partner,
            device_id_type=MESH,
        ).wait_recv()

    def sent(src, s):
        pltpu.make_async_remote_copy(
            src_ref=src,
            dst_ref=src,
            send_sem=ssem.at[s],
            recv_sem=rsem.at[0],
            device_id=partner,
            device_id_type=MESH,
        ).wait_send()

    rows_in = ph.shape[0] // P_CHUNKS

    def load(k):
        at = pl.ds(k * rows_in, rows_in)
        return pltpu.make_async_copy(passage_hbm.at[at], ph.at[at], lsem.at[L_IN + k])

    def unload(k):
        at = pl.ds(k * rows_in, rows_in)
        return pltpu.make_async_copy(gp_buf.at[at], gp_hbm.at[at], lsem.at[L_OUT + k])

    for k in range(P_CHUNKS):
        load(k).start()

    barrier = pltpu.get_barrier_semaphore()
    peers = [in_group(*r) for r in GROUP_RELATIVE[1:]]
    peers += [in_dp(dl, dy) for dl in range(4) for dy in range(4) if (dl, dy) != (0, 0)]
    peers += [{"zh": 1 - zh, "zl": lax.rem(zl + d, 4)} for d in range(1, 4)]
    for peer in peers:
        pl.semaphore_signal(barrier, inc=1, device_id=peer, device_id_type=MESH)

    pre = jnp.dot(query_hidden[...], projection[...], preferred_element_type=F32)
    q_pre[...] = pre
    scale = lax.rsqrt(jnp.sum(pre * pre, axis=-1, keepdims=True) + norm_eps)
    qg[0] = (pre * scale).astype(BF16)

    lanes = lax.broadcasted_iota(jnp.int32, (8, 128), 1)
    rows = lax.broadcasted_iota(jnp.int32, (8, 128), 0)
    chosen_row = jnp.zeros((8, 128), F32)
    for k in range(8):
        chosen_row = jnp.where(rows == k, positive[k].astype(F32), chosen_row)
    meta[0] = jnp.where(lanes == 32, chosen_row, 0.0)
    meta[0, :, 0:32] = hard_ids[...].astype(F32)

    pl.semaphore_wait(barrier, len(peers))

    push(qg.at[0], qg.at[slot_of(1, 0, 0)], S_GATHER, R_GATHER + slot_of(1, 0, 0), across)
    for n, d in enumerate((2, 1, 3)):
        to = slot_of(0, back(d, 4), 0)
        push(qg.at[0], qg.at[to], S_GATHER + 1 + n, R_GATHER + to, at_x(d))
    push(qg.at[0], qg.at[1], S_GATHER + 4, R_GATHER + 1, partner)
    for dz, dx, dc in GROUP_RELATIVE[1:]:
        to = slot_of(dz, back(dx, 4), dc)
        push(
            meta.at[0],
            meta.at[to],
            S_META + slot_of(dz, dx, dc),
            R_META + to,
            in_group(dz, dx, dc),
        )

    for k in range(P_CHUNKS):
        load(k).wait()
        at = pl.ds(k * rows_in, rows_in)
        pre = jnp.dot(ph[at, :], projection[...], preferred_element_type=F32)
        p_pre[at, :] = pre
        scale = lax.rsqrt(jnp.sum(pre * pre, axis=-1, keepdims=True) + norm_eps)
        unit = (pre * scale).astype(BF16)
        pe[at, :] = unit
        pe_t[:, at] = unit.T
    qh_t[...] = query_hidden[...].T

    def relay_x(dz, first):
        for n, d in enumerate((1, 2, 3)):
            here, there = slot_of(dz, d, 0), slot_of(dz, d, 1)
            arrived(qg.at[here], R_GATHER + here)
            push(qg.at[here], qg.at[there], first + n, R_GATHER + there, partner)

    def relay_z():
        here = slot_of(1, 0, 0)
        arrived(qg.at[here], R_GATHER + here)
        for n, d in enumerate((2, 1, 3)):
            to = slot_of(1, back(d, 4), 0)
            push(qg.at[here], qg.at[to], S_GATHER + 8 + n, R_GATHER + to, at_x(d))
        push(qg.at[here], qg.at[here + 1], S_GATHER + 11, R_GATHER + here + 1, partner)

    def count_hard():
        for dz, dx, dc in GROUP_RELATIVE:
            slot = slot_of(dz, dx, dc)
            if slot:
                arrived(meta.at[slot], R_META + slot)
            first = pl.multiple_of(group_of(dz, dx, dc) * 8, 8)
            meta_rows[pl.ds(first, 8), :] = meta[slot]
        turned = meta_rows[...].T
        own = (
            group_of(0, 0, 0) * 16 + lax.broadcasted_iota(jnp.int32, (16, 128), 0)
        ).astype(F32)
        counts = jnp.zeros((16, 128), F32)
        for k in range(32):
            counts += (turned[k : k + 1, :] == own).astype(F32)
        counts_ref[...] = counts
        chosen_ref[...] = (turned[32:33, :] == own).astype(F32)

    passages = sums.shape[1]
    step = 4
    height = step * 128

    def forward(k, carry):
        @pl.when(k == 1)
        def _():
            relay_x(0, S_GATHER + 5)

        @pl.when(k == 4)
        def _():
            relay_z()

        @pl.when(k == 6)
        def _():
            count_hard()

        @pl.when(k == 10)
        def _():
            relay_x(1, S_GATHER + 12)

        @pl.when(lax.rem(k, 2) == 1)
        def _():
            arrived(qg.at[k], R_GATHER + k)

        block = qg[k]
        for n in range(passages // step):
            similar = contract_last(pe[n * height : (n + 1) * height, :], block)
            grown = jnp.exp2(similar * EXP2_SCALE)
            for i in range(step):
                p = n * step + i
                token = lax.broadcasted_iota(jnp.int32, (128, grown.shape[1]), 0)
                live = jnp.where(token < plen[p], grown[i * 128 : (i + 1) * 128], 0.0)
                e_ref[k, p * 128 : (p + 1) * 128, :] = live.astype(BF16)
                sums[k, p : p + 1, :] = jnp.sum(live, axis=0, keepdims=True)
        return carry

    lax.fori_loop(0, 16, forward, 0)

    tokens = sums.shape[2]
    every = sums[...].reshape(16 * passages, tokens)
    spread_from = (
        lax.broadcasted_iota(jnp.int32, (tokens, 128), 0) // 32
        == lax.rem(lax.broadcasted_iota(jnp.int32, (tokens, 128), 1), 8)
    ).astype(F32)
    spread_to = (
        lax.broadcasted_iota(jnp.int32, (128, tokens), 1) // 32
        == lax.rem(lax.broadcasted_iota(jnp.int32, (128, tokens), 0), 8)
    ).astype(F32)
    per_slot = jnp.dot(
        0.1 * jnp.log(every), spread_from, precision=HIGHEST, preferred_element_type=F32
    )
    lane_group = lax.broadcasted_iota(jnp.int32, (passages, 128), 1) // 8
    scores = jnp.zeros((passages, 128), F32)
    for dz, dx, dc in GROUP_RELATIVE:
        slot = slot_of(dz, dx, dc)
        part = per_slot[slot * passages : (slot + 1) * passages]
        scores += jnp.where(lane_group == group_of(dz, dx, dc), part, 0.0)

    counts, chosen = counts_ref[...], chosen_ref[...]
    grown = jnp.exp(scores - SHIFT)
    hard = counts * grown
    other_hard = jnp.where(chosen > 0.5, 0.0, hard)
    score_ref[...] = scores
    st_send[...] = jnp.zeros_like(st_send)
    st_send[0:1, :] = jnp.sum(grown, axis=0, keepdims=True)
    st_send[1:2, :] = jnp.sum(other_hard * grown, axis=0, keepdims=True)
    st_send[2:3, :] = jnp.sum(chosen * scores, axis=0, keepdims=True)
    st_send[3:4, :] = jnp.sum(hard, axis=0, keepdims=True)
    for dz, dx, dc in GROUP_RELATIVE[1:]:
        to = slot_of(dz, back(dx, 4), dc)
        push(
            st_send,
            st_recv.at[to],
            S_STATS + slot_of(dz, dx, dc),
            R_STATS + to,
            in_group(dz, dx, dc),
        )
    stats = st_send[...]
    for slot in range(1, 16):
        arrived(st_recv.at[slot], R_STATS + slot)
        stats += st_recv[slot]
    h_send[...] = stats
    for dl in range(4):
        for dy in range(4):
            if (dl, dy) != (0, 0):
                to = back(dl, 4) * 4 + back(dy, 4)
                push(
                    h_send,
                    h_recv.at[to],
                    S_HARD + dl * 4 + dy,
                    R_HARD + to,
                    in_dp(dl, dy),
                )
    total = stats[3:4, :]
    for slot in range(1, 16):
        arrived(h_recv.at[slot], R_HARD + slot)
        total += h_recv[slot, 3:4, :]
    boost = (8.0 * 65536.0) / jnp.sum(total, axis=1, keepdims=True)
    partition = stats[0:1, :] + boost * stats[1:2, :]
    loss = jnp.log(partition) + SHIFT - stats[2:3, :]
    own_lane = lanes == group_of(0, 0, 0) * 8 + rows
    losses_out[...] = jnp.broadcast_to(
        jnp.sum(jnp.where(own_lane, loss, 0.0), axis=1, keepdims=True), (8, 128)
    )
    score_grad = grown * (1.0 + boost * other_hard) / partition - chosen

    picked = [
        jnp.where(lane_group == group_of(dz, dx, dc), score_grad, 0.0)
        for dz, dx, dc in GROUP_RELATIVE
    ]
    spread = jnp.dot(
        jnp.concatenate(picked, axis=0),
        spread_to,
        precision=HIGHEST,
        preferred_element_type=F32,
    )
    w_ref[...] = (spread / every).reshape(w_ref.shape)
    pg[...] = jnp.zeros_like(pg)

    def combine(j):
        arrived(rc.at[j], R_QC + j)
        both = qgt[2 * j + 1].astype(F32) + rc[j].astype(F32)
        side = j // 4
        d = lax.rem(j + 1, 4)

        @pl.when(d != 0)
        def _():
            cs[j] = both.astype(BF16)
            to = side * 4 + (4 - d)
            push(cs.at[j], rx.at[to], S_QX + j, R_QX + to, {"x": lax.rem(x + d, 4)})

        @pl.when(d == 0)
        def _():
            own_c[side] = both

    def over_x(side):
        whole = own_c[side]
        for d in range(1, 4):
            arrived(rx.at[side * 4 + d], R_QX + side * 4 + d)
            whole += rx[side * 4 + d].astype(F32)
        return whole

    def backward(it, carry):
        j = it // 2
        dz = 1 - j // 4
        dx = lax.rem(j + 1, 4)
        dc = 1 - lax.rem(it, 2)
        k = dz * 8 + dx * 2 + dc
        block = qg[k]
        acc = None
        for n in range(passages // step):
            parts = []
            for i in range(step):
                p = n * step + i
                weight = w_ref[k, p : p + 1, :]
                kept = e_ref[k, p * 128 : (p + 1) * 128, :].astype(F32)
                parts.append((kept * weight).astype(BF16))
            coefficient = jnp.concatenate(parts, axis=0)
            at = slice(n * height, (n + 1) * height)
            pg[at, :] += jnp.dot(coefficient, block, preferred_element_type=F32)
            term = jnp.dot(pe_t[:, at], coefficient, preferred_element_type=F32)
            acc = term if acc is None else acc + term
        qgt[it] = acc.astype(BF16)

        @pl.when(dc == 1)
        def _():
            push(qgt.at[it], rc.at[j], S_QC + j, R_QC + j, partner)

            @pl.when(it >= 2)
            def _():
                combine(j - 1)

        @pl.when(it == 13)
        def _():
            zs[...] = over_x(0).astype(BF16)
            push(zs, rz, S_QZ, R_QZ, across)

        return carry

    lax.fori_loop(0, 16, backward, 0)
    combine(7)

    w_t = jnp.zeros((128, ph.shape[1]), F32)
    for k in range(P_CHUNKS):
        at = pl.ds(k * rows_in, rows_in)
        pb = norm_vjp(p_pre[at, :], pg[at, :]).astype(BF16)
        pb_t[:, at] = pb.T
        gp_buf[at, :] = contract_last(pb, projection[...]).astype(BF16)
        unload(k).start()
    w_t = jnp.dot(pb_t[...], ph[...], preferred_element_type=F32)
    w_loc[...] = w_t.T

    arrived(rz, R_QZ)
    whole = over_x(1) + rz[...].astype(F32)
    qb = norm_vjp(q_pre[...], whole.T).astype(BF16)
    w_loc[...] += jnp.dot(qh_t[...], qb, preferred_element_type=F32)

    half = w_loc.shape[0] // 2
    quarter = half // 4
    piece = quarter // 4

    def rows_at(first, count):
        return pl.ds(pl.multiple_of(first, 8), count)

    push(w_loc.at[rows_at((1 - c) * half, half)], ac_recv, S_AC, R_AC, partner)
    gq_out[...] = contract_last(qb, projection[...]).astype(BF16)
    arrived(ac_recv, R_AC)
    h_core[...] = w_loc[rows_at(c * half, half), :] + ac_recv[...]
    for d in (2, 1, 3):
        push(
            h_core.at[rows_at(lax.rem(x + d, 4) * quarter, quarter)],
            ax_recv.at[4 - d],
            S_AX + d,
            R_AX + 4 - d,
            at_x(d),
        )
    mine = h_core[rows_at(x * quarter, quarter), :]
    for d in range(1, 4):
        arrived(ax_recv.at[d], R_AX + d)
        mine += ax_recv[d]
    h_x[...] = mine
    for d in (2, 1, 3):
        push(
            h_x.at[rows_at(lax.rem(y + d, 4) * piece, piece)],
            ay_recv.at[4 - d],
            S_AY + d,
            R_AY + 4 - d,
            at_y(d),
        )
    mine = h_x[rows_at(y * piece, piece), :]
    for d in range(1, 4):
        arrived(ay_recv.at[d], R_AY + d)
        mine += ay_recv[d]
    h_y[...] = mine
    for d in (4, 3, 5, 2, 6, 1, 7):
        push(h_y, az_recv.at[z], S_AZ + d, R_AZ + 8 - d, at_z(d))
    az_recv[z] = mine
    for d in range(1, 8):
        arrived(az_recv.at[0], R_AZ + d)
    mine = az_recv[0]
    for k in range(1, 8):
        mine += az_recv[k]
    base = c * half + x * quarter
    own_rows = rows_at(base + y * piece, piece)
    fin[own_rows, :] = mine
    for d in (2, 1, 3):
        push(fin.at[own_rows], fin.at[own_rows], S_GY + d, R_GY + 4 - d, at_y(d))
    for d in range(1, 4):
        arrived(fin.at[own_rows], R_GY + d)
    own_rows = rows_at(base, quarter)
    for d in (2, 1, 3):
        push(fin.at[own_rows], fin.at[own_rows], S_GX + d, R_GX + 4 - d, at_x(d))
    for d in range(1, 4):
        arrived(fin.at[own_rows], R_GX + d)
    own_rows = rows_at(c * half, half)
    push(fin.at[own_rows], fin.at[own_rows], S_GC, R_GC, partner)
    arrived(fin.at[own_rows], R_GC)
    proj_out[...] = fin[...]

    for n in range(15):
        sent(qg.at[0], S_GATHER + n)
    for n in range(1, 16):
        sent(meta.at[0], S_META + n)
        sent(st_send, S_STATS + n)
        sent(h_send, S_HARD + n)
    for n in range(8):
        sent(qgt.at[0], S_QC + n)
        if n % 4 != 3:
            sent(cs.at[0], S_QX + n)
    sent(zs, S_QZ)
    sent(ac_recv, S_AC)
    for d in range(1, 4):
        sent(ax_recv.at[0], S_AX + d)
        sent(ay_recv.at[0], S_AY + d)
        sent(h_y, S_GY + d)
        sent(h_x, S_GX + d)
    for d in range(1, 8):
        sent(h_y, S_AZ + d)
    sent(ac_recv, S_GC)
    for k in range(P_CHUNKS):
        unload(k).wait()


def local(query_hidden, passage_hidden, projection, positive, hard_ids, passage_len):
    queries, query_len, width = query_hidden.shape
    passages, slots, _ = passage_hidden.shape
    dim = projection.shape[1]
    q_rows, p_rows = queries * query_len, passages * slots
    half = width // 2
    quarter = half // 4
    piece = quarter // 4
    vmem = pl.BlockSpec(memory_space=pltpu.VMEM)
    smem = pl.BlockSpec(memory_space=pltpu.SMEM)
    hbm = pl.BlockSpec(memory_space=pl.ANY)
    scratch = [
        pltpu.VMEM((p_rows, width), BF16),
        pltpu.VMEM((q_rows, dim), F32),
        pltpu.VMEM((p_rows, dim), F32),
        pltpu.VMEM((p_rows, dim), BF16),
        pltpu.VMEM((dim, p_rows), BF16),
        pltpu.VMEM((width, q_rows), BF16),
        pltpu.VMEM((16, q_rows, dim), BF16),
        pltpu.VMEM((16, p_rows, q_rows), BF16),
        pltpu.VMEM((16, passages, q_rows), F32),
        pltpu.VMEM((16, passages, q_rows), F32),
        pltpu.VMEM((p_rows, dim), F32),
        pltpu.VMEM((16, 8, 128), F32),
        pltpu.VMEM((128, 128), F32),
        pltpu.VMEM((passages, 128), F32),
        pltpu.VMEM((passages, 128), F32),
        pltpu.VMEM((passages, 128), F32),
        pltpu.VMEM((8, 128), F32),
        pltpu.VMEM((16, 8, 128), F32),
        pltpu.VMEM((8, 128), F32),
        pltpu.VMEM((16, 8, 128), F32),
        pltpu.VMEM((16, dim, q_rows), BF16),
        pltpu.VMEM((8, dim, q_rows), BF16),
        pltpu.VMEM((8, dim, q_rows), BF16),
        pltpu.VMEM((2, dim, q_rows), F32),
        pltpu.VMEM((8, dim, q_rows), BF16),
        pltpu.VMEM((dim, q_rows), BF16),
        pltpu.VMEM((dim, q_rows), BF16),
        pltpu.VMEM((dim, p_rows), BF16),
        pltpu.VMEM((p_rows, width), BF16),
        pltpu.VMEM((width, dim), F32),
        pltpu.VMEM((half, dim), F32),
        pltpu.VMEM((half, dim), F32),
        pltpu.VMEM((4, quarter, dim), F32),
        pltpu.VMEM((quarter, dim), F32),
        pltpu.VMEM((4, piece, dim), F32),
        pltpu.VMEM((piece, dim), F32),
        pltpu.VMEM((8, piece, dim), F32),
        pltpu.VMEM((width, dim), F32),
        pltpu.SemaphoreType.DMA((SEND.total,)),
        pltpu.SemaphoreType.DMA((RECV.total,)),
        pltpu.SemaphoreType.DMA((LOCAL.total,)),
    ]
    losses, grad_proj, grad_query, grad_passage = pl.pallas_call(
        kernel,
        out_shape=(
            jax.ShapeDtypeStruct((8, 128), F32),
            jax.ShapeDtypeStruct((width, dim), F32),
            jax.ShapeDtypeStruct((q_rows, width), BF16),
            jax.ShapeDtypeStruct((p_rows, width), BF16),
        ),
        in_specs=[smem, smem, vmem, hbm, vmem, vmem],
        out_specs=(vmem, vmem, vmem, hbm),
        scratch_shapes=scratch,
        compiler_params=pltpu.CompilerParams(
            collective_id=0, has_side_effects=True, vmem_limit_bytes=60 << 20
        ),
        name="late_interaction_step",
    )(
        passage_len,
        positive,
        query_hidden.reshape(q_rows, width),
        passage_hidden.reshape(p_rows, width),
        projection,
        hard_ids,
    )
    return (
        losses[:, 0],
        grad_proj,
        grad_query.reshape(query_hidden.shape),
        grad_passage.reshape(passage_hidden.shape),
    )


def solution(mesh):
    split = Mesh(mesh.devices.reshape(2, 4, 2, 4, 4), AXES)
    placed = (
        P(SPLIT, None, None),
        P(SPLIT, None, None),
        P(),
        P(SPLIT),
        P(SPLIT, None),
        P(SPLIT),
    )
    return jax.shard_map(
        local,
        mesh=split,
        in_specs=placed,
        out_specs=(P(SPLIT), P(), P(SPLIT, None, None), P(SPLIT, None, None)),
        check_vma=False,
    )
```

time: 659 us -> 92.8 us (0.14)
  waiting for transfers between devices: 298 us -> 0 us
  matrix products: 116 us -> 0 us
  Pallas kernels: 0 us -> 83.3 us
  other arithmetic: 82.1 us -> 0 us
  blocking collectives: 51.8 us -> 0 us
  local copies, waits for them, and re-layouts: 59.9 us -> 8.66 us
  starting transfers between devices: 31.7 us -> 0 us
  between operations: 15 us -> 0.64 us
    psum x1 -> x0, waiting for transfers between devices: 246 us -> none  [local(): grad_proj = lax.psum(local_weight, GROUP_DP)]
    dot_general x70 -> x0, matrix products: 116 us -> none  [the longest x34 58.5 us: contract_last(): lax.dot_general(left, right, (((1,), (1,)), ((), ())), preferred_element_...]
    pallas_call x0 -> x1, Pallas kernels: none -> 83.3 us  [local(): pl.pallas_call(kernel, out_shape=(jax.ShapeDtypeStruct((8, 128), F32), ja...]
    all_to_all x4 -> x0, waiting for transfers between devices: 52.3 us -> none  [the longest x1 18.9 us: summed_on_arrival(): lax.all_to_all(cut_along(array, dim, devices), axis, 0, 0, tiled=True)]
    psum x5 -> x0, blocking collectives: 43.2 us -> none  [one_axis_at_a_time(): array = lax.psum(array, axis)]
    add x16 -> x0, other arithmetic: 40.5 us -> none  [backward_block(): return (running + rounded.astype(jnp.float32), query_part)]
    all_to_all x4 -> x0, starting transfers between devices: 31.7 us -> none  [the longest x1 12.4 us: copy_for_each(): return lax.all_to_all(copies, axis, split_axis=0, concat_axis=0, tiled=True)]
    while x98 -> x0, local copies, waits for them, and re-layouts: 20.1 us -> none
  transfers between devices with their start and end apart: 5 -> 0, of which waited for: 5 -> 0; matrix products, arithmetic and copies ran while one was open for 2% -> 0% of each run, Pallas kernels for 0% -> 0%
where the time goes in v1:
time: 92.8 us; the launch traced here: 92.6 us
  Pallas kernels  83.3 us (90%)
  local copies, waits for them, and re-layouts  8.66 us (9%)
    pallas_call x1, Pallas kernels, local(): pl.pallas_call(kernel, out_shape=(jax.ShapeDtypeStruct((8, 128), F32), ja...  83.3 us
    unnamed x3, local copies, waits for them, and re-layouts  7.36 us

profile of v1, /device:TPU:1, one launch (start us, length us, event | category | flops | bytes accessed | tf_op | source)
XLA Modules:
  0.0 92.6 jit_solution(7261129867470559186)
XLA Ops:
  0.6 83.3 %late_interaction_step.1 = (f32[8,128]{1,0:T(8,128)}, f32[768,128]{1,0:T(8,128)}, bf16[256,768]{1,0:T(8,128)(2,1)}, bf16[2048,768]{1,0:T(8,128)(2,1)}) custom-call(s32[16]{0:T(128)} %plen.1, s32[8]{0:T(128)} %positive.1, bf16[256,768]{1,0:T(8,128)(2,1)} %bitcast.6, bf16[2048,768]{1,0:T(8,128)(2,1)} %bitcast.4, bf16[768,128]{1,0:T(8,128)(2,1)} %projection.1, ...), custom_call_target="tpu_custom_call" | custom-call | tf_op jit(solution)/shard_map/late_interaction_step/pallas_call | solution.py:616
  83.9 1.3 %slice_reduce_fusion = f32[8]{0:T(128)} fusion(f32[8,128]{1,0:T(8,128)} %get-tuple-element.8), kind=kLoop, calls=%fused_computation | loop fusion | bytes 64 | tf_op jit(solution)/shard_map/slice | solution.py:640
  85.2 1.8 %copy.13 = f32[768,128]{1,0:T(8,128)} copy(f32[768,128]{1,0:T(8,128)} %get-tuple-element.17) | data formatting | bytes 786432
  87.0 1.8 %copy.14 = bf16[8,32,768]{2,1,0:T(8,128)(2,1)} copy(bf16[8,32,768]{2,1,0:T(8,128)(2,1)} %bitcast.7) | data formatting | bytes 786432
  88.7 3.8 %copy.15 = bf16[16,128,768]{2,1,0:T(8,128)(2,1)} copy(bf16[16,128,768]{2,1,0:T(8,128)(2,1)} %bitcast.5) | data formatting | bytes 6291456

commit v2 on v1

--- a/solution.py
+++ b/solution.py
@@ -21,6 +21,8 @@
 
 GROUP_RELATIVE = [(dz, dx, dc) for dz in range(2) for dx in range(4) for dc in range(2)]
 
+PLANE_RELATIVE = [(dx, dc, dy) for dx in range(4) for dc in range(2) for dy in range(4)]
+
 
 def slot_of(dz, dx, dc):
     return dz * 8 + dx * 2 + dc
@@ -58,7 +60,8 @@
 S_GATHER, R_GATHER = SEND.take(15), RECV.take(16)
 S_META, R_META = SEND.take(16), RECV.take(16)
 S_STATS, R_STATS = SEND.take(16), RECV.take(16)
-S_HARD, R_HARD = SEND.take(16), RECV.take(16)
+S_HARD, R_HARD = SEND.take(32), RECV.take(32)
+S_HZ, R_HZ = SEND.take(8), RECV.take(8)
 S_QC, R_QC = SEND.take(8), RECV.take(8)
 S_QX, R_QX = SEND.take(8), RECV.take(8)
 S_QZ, R_QZ = SEND.take(1), RECV.take(1)
@@ -70,8 +73,8 @@
 S_GX, R_GX = SEND.take(4), RECV.take(4)
 S_GC, R_GC = SEND.take(1), RECV.take(1)
 P_CHUNKS = 4
+OUT_CHUNKS = 4
 L_IN = LOCAL.take(P_CHUNKS)
-L_OUT = LOCAL.take(P_CHUNKS)
 
 
 def kernel(
@@ -82,9 +85,9 @@
     projection,
     hard_ids,
     losses_out,
-    proj_out,
-    gq_out,
-    gp_hbm,
+    fin,
+    qb_out,
+    pb_out,
     ph,
     q_pre,
     p_pre,
@@ -103,8 +106,8 @@
     score_ref,
     st_send,
     st_recv,
-    h_send,
     h_recv,
+    hz_recv,
     qgt,
     rc,
     cs,
@@ -113,8 +116,8 @@
     zs,
     rz,
     pb_t,
-    gp_buf,
     w_loc,
+    w_send,
     ac_recv,
     h_core,
     ax_recv,
@@ -122,7 +125,7 @@
     ay_recv,
     h_y,
     az_recv,
-    fin,
+    parts,
     ssem,
     rsem,
     lsem,
@@ -144,8 +147,8 @@
     def in_group(dz, dx, dc):
         return {"zh": lax.rem(zh + dz, 2), "x": lax.rem(x + dx, 4), "c": lax.rem(c + dc, 2)}
 
-    def in_dp(dl, dy):
-        return {"zl": lax.rem(zl + dl, 4), "y": lax.rem(y + dy, 4)}
+    def in_plane(dx, dc, dy):
+        return {"x": lax.rem(x + dx, 4), "c": lax.rem(c + dc, 2), "y": lax.rem(y + dy, 4)}
 
     partner = {"c": 1 - c}
     across = {"zh": 1 - zh}
@@ -189,17 +192,13 @@
         at = pl.ds(k * rows_in, rows_in)
         return pltpu.make_async_copy(passage_hbm.at[at], ph.at[at], lsem.at[L_IN + k])
 
-    def unload(k):
-        at = pl.ds(k * rows_in, rows_in)
-        return pltpu.make_async_copy(gp_buf.at[at], gp_hbm.at[at], lsem.at[L_OUT + k])
-
     for k in range(P_CHUNKS):
         load(k).start()
 
     barrier = pltpu.get_barrier_semaphore()
     peers = [in_group(*r) for r in GROUP_RELATIVE[1:]]
-    peers += [in_dp(dl, dy) for dl in range(4) for dy in range(4) if (dl, dy) != (0, 0)]
-    peers += [{"zh": 1 - zh, "zl": lax.rem(zl + d, 4)} for d in range(1, 4)]
+    peers += [in_plane(*r) for r in PLANE_RELATIVE[1:] if r[2]]
+    peers += [at_z(d) for d in range(1, 8) if d != 4]
     for peer in peers:
         pl.semaphore_signal(barrier, inc=1, device_id=peer, device_id_type=MESH)
 
@@ -279,27 +278,7 @@
     step = 4
     height = step * 128
 
-    def forward(k, carry):
-        @pl.when(k == 1)
-        def _():
-            relay_x(0, S_GATHER + 5)
-
-        @pl.when(k == 4)
-        def _():
-            relay_z()
-
-        @pl.when(k == 6)
-        def _():
-            count_hard()
-
-        @pl.when(k == 10)
-        def _():
-            relay_x(1, S_GATHER + 12)
-
-        @pl.when(lax.rem(k, 2) == 1)
-        def _():
-            arrived(qg.at[k], R_GATHER + k)
-
+    def grow(k):
         block = qg[k]
         for n in range(passages // step):
             similar = contract_last(pe[n * height : (n + 1) * height, :], block)
@@ -310,9 +289,31 @@
                 live = jnp.where(token < plen[p], grown[i * 128 : (i + 1) * 128], 0.0)
                 e_ref[k, p * 128 : (p + 1) * 128, :] = live.astype(BF16)
                 sums[k, p : p + 1, :] = jnp.sum(live, axis=0, keepdims=True)
+
+    grow(0)
+    relay_x(0, S_GATHER + 5)
+    arrived(qg.at[1], R_GATHER + 1)
+    grow(1)
+
+    def forward(t, carry):
+        @pl.when(t == 2)
+        def _():
+            relay_z()
+
+        @pl.when(t == 3)
+        def _():
+            count_hard()
+
+        @pl.when(t == 5)
+        def _():
+            relay_x(1, S_GATHER + 12)
+
+        arrived(qg.at[2 * t + 1], R_GATHER + 2 * t + 1)
+        grow(2 * t)
+        grow(2 * t + 1)
         return carry
 
-    lax.fori_loop(0, 16, forward, 0)
+    lax.fori_loop(1, 8, forward, 0)
 
     tokens = sums.shape[2]
     every = sums[...].reshape(16 * passages, tokens)
@@ -343,7 +344,12 @@
     st_send[0:1, :] = jnp.sum(grown, axis=0, keepdims=True)
     st_send[1:2, :] = jnp.sum(other_hard * grown, axis=0, keepdims=True)
     st_send[2:3, :] = jnp.sum(chosen * scores, axis=0, keepdims=True)
-    st_send[3:4, :] = jnp.sum(hard, axis=0, keepdims=True)
+    h_recv[0:1, :] = jnp.sum(hard, axis=0, keepdims=True)
+    own = h_recv.at[pl.ds(0, 1)]
+    for dx, dc, dy in PLANE_RELATIVE[1:]:
+        at = dx * 8 + dc * 4 + dy
+        to = back(dx, 4) * 8 + dc * 4 + back(dy, 4)
+        push(own, h_recv.at[pl.ds(to, 1)], S_HARD + at, R_HARD + to, in_plane(dx, dc, dy))
     for dz, dx, dc in GROUP_RELATIVE[1:]:
         to = slot_of(dz, back(dx, 4), dc)
         push(
@@ -353,26 +359,19 @@
             R_STATS + to,
             in_group(dz, dx, dc),
         )
+    for n in range(1, 32):
+        arrived(h_recv.at[pl.ds(n, 1)], R_HARD + n)
+    hz_recv[0:1, :] = jnp.sum(h_recv[...], axis=0, keepdims=True)
+    own = hz_recv.at[pl.ds(0, 1)]
+    for d in (4, 3, 5, 2, 6, 1, 7):
+        push(own, hz_recv.at[pl.ds(8 - d, 1)], S_HZ + d, R_HZ + 8 - d, at_z(d))
     stats = st_send[...]
     for slot in range(1, 16):
         arrived(st_recv.at[slot], R_STATS + slot)
         stats += st_recv[slot]
-    h_send[...] = stats
-    for dl in range(4):
-        for dy in range(4):
-            if (dl, dy) != (0, 0):
-                to = back(dl, 4) * 4 + back(dy, 4)
-                push(
-                    h_send,
-                    h_recv.at[to],
-                    S_HARD + dl * 4 + dy,
-                    R_HARD + to,
-                    in_dp(dl, dy),
-                )
-    total = stats[3:4, :]
-    for slot in range(1, 16):
-        arrived(h_recv.at[slot], R_HARD + slot)
-        total += h_recv[slot, 3:4, :]
+    for n in range(1, 8):
+        arrived(hz_recv.at[pl.ds(n, 1)], R_HZ + n)
+    total = jnp.sum(hz_recv[...], axis=0, keepdims=True)
     boost = (8.0 * 65536.0) / jnp.sum(total, axis=1, keepdims=True)
     partition = stats[0:1, :] + boost * stats[1:2, :]
     loss = jnp.log(partition) + SHIFT - stats[2:3, :]
@@ -458,20 +457,21 @@
     lax.fori_loop(0, 16, backward, 0)
     combine(7)
 
-    w_t = jnp.zeros((128, ph.shape[1]), F32)
     for k in range(P_CHUNKS):
         at = pl.ds(k * rows_in, rows_in)
         pb = norm_vjp(p_pre[at, :], pg[at, :]).astype(BF16)
         pb_t[:, at] = pb.T
-        gp_buf[at, :] = contract_last(pb, projection[...]).astype(BF16)
-        unload(k).start()
+        pb_out[at, :] = pb
     w_t = jnp.dot(pb_t[...], ph[...], preferred_element_type=F32)
     w_loc[...] = w_t.T
 
     arrived(rz, R_QZ)
     whole = over_x(1) + rz[...].astype(F32)
     qb = norm_vjp(q_pre[...], whole.T).astype(BF16)
-    w_loc[...] += jnp.dot(qh_t[...], qb, preferred_element_type=F32)
+    qb_out[...] = qb
+    whole = w_loc[...] + jnp.dot(qh_t[...], qb, preferred_element_type=F32)
+    w_loc[...] = whole
+    w_send[...] = whole.astype(BF16)
 
     half = w_loc.shape[0] // 2
     quarter = half // 4
@@ -480,10 +480,11 @@
     def rows_at(first, count):
         return pl.ds(pl.multiple_of(first, 8), count)
 
-    push(w_loc.at[rows_at((1 - c) * half, half)], ac_recv, S_AC, R_AC, partner)
-    gq_out[...] = contract_last(qb, projection[...]).astype(BF16)
+    push(w_send.at[rows_at((1 - c) * half, half)], ac_recv, S_AC, R_AC, partner)
     arrived(ac_recv, R_AC)
-    h_core[...] = w_loc[rows_at(c * half, half), :] + ac_recv[...]
+    mine = w_loc[rows_at(c * half, half), :] + ac_recv[...].astype(F32)
+    w_loc[rows_at(c * half, half), :] = mine
+    h_core[...] = mine.astype(BF16)
     for d in (2, 1, 3):
         push(
             h_core.at[rows_at(lax.rem(x + d, 4) * quarter, quarter)],
@@ -492,10 +493,11 @@
             R_AX + 4 - d,
             at_x(d),
         )
-    mine = h_core[rows_at(x * quarter, quarter), :]
-    for d in range(1, 4):
+    base = c * half + x * quarter
+    mine = w_loc[rows_at(base, quarter), :]
+    for d in (1, 3, 2):
         arrived(ax_recv.at[d], R_AX + d)
-        mine += ax_recv[d]
+        mine += ax_recv[d].astype(F32)
     h_x[...] = mine
     for d in (2, 1, 3):
         push(
@@ -506,41 +508,45 @@
             at_y(d),
         )
     mine = h_x[rows_at(y * piece, piece), :]
-    for d in range(1, 4):
+    for d in (1, 3, 2):
         arrived(ay_recv.at[d], R_AY + d)
         mine += ay_recv[d]
-    h_y[...] = mine
+    h_y[...] = mine.astype(BF16)
     for d in (4, 3, 5, 2, 6, 1, 7):
         push(h_y, az_recv.at[z], S_AZ + d, R_AZ + 8 - d, at_z(d))
-    az_recv[z] = mine
+    az_recv[z] = h_y[...]
     for d in range(1, 8):
         arrived(az_recv.at[0], R_AZ + d)
-    mine = az_recv[0]
+    mine = az_recv[0].astype(F32)
     for k in range(1, 8):
-        mine += az_recv[k]
-    base = c * half + x * quarter
-    own_rows = rows_at(base + y * piece, piece)
-    fin[own_rows, :] = mine
+        mine += az_recv[k].astype(F32)
+    place = (c * 4 + x) * 4
+    parts[place + y] = mine.astype(BF16)
+    own = parts.at[place + y]
     for d in (2, 1, 3):
-        push(fin.at[own_rows], fin.at[own_rows], S_GY + d, R_GY + 4 - d, at_y(d))
+        push(own, own, S_GY + d, R_GY + 4 - d, at_y(d))
     for d in range(1, 4):
-        arrived(fin.at[own_rows], R_GY + d)
-    own_rows = rows_at(base, quarter)
+        arrived(own, R_GY + d)
+    own = parts.at[pl.ds(place, 4)]
     for d in (2, 1, 3):
-        push(fin.at[own_rows], fin.at[own_rows], S_GX + d, R_GX + 4 - d, at_x(d))
+        push(own, own, S_GX + d, R_GX + 4 - d, at_x(d))
     for d in range(1, 4):
-        arrived(fin.at[own_rows], R_GX + d)
-    own_rows = rows_at(c * half, half)
-    push(fin.at[own_rows], fin.at[own_rows], S_GC, R_GC, partner)
-    arrived(fin.at[own_rows], R_GC)
-    proj_out[...] = fin[...]
+        arrived(own, R_GX + d)
+    own = parts.at[pl.ds(c * 16, 16)]
+    push(own, own, S_GC, R_GC, partner)
+    arrived(own, R_GC)
+    for k in range(32):
+        fin[k * piece : (k + 1) * piece, :] = parts[k].astype(F32)
 
     for n in range(15):
         sent(qg.at[0], S_GATHER + n)
     for n in range(1, 16):
         sent(meta.at[0], S_META + n)
         sent(st_send, S_STATS + n)
-        sent(h_send, S_HARD + n)
+    for n in range(1, 32):
+        sent(h_recv.at[pl.ds(0, 1)], S_HARD + n)
+    for n in range(1, 8):
+        sent(hz_recv.at[pl.ds(0, 1)], S_HZ + n)
     for n in range(8):
         sent(qgt.at[0], S_QC + n)
         if n % 4 != 3:
@@ -550,12 +556,31 @@
     for d in range(1, 4):
         sent(ax_recv.at[0], S_AX + d)
         sent(ay_recv.at[0], S_AY + d)
-        sent(h_y, S_GY + d)
-        sent(h_x, S_GX + d)
+        sent(parts.at[0], S_GY + d)
+        sent(parts.at[pl.ds(0, 4)], S_GX + d)
     for d in range(1, 8):
         sent(h_y, S_AZ + d)
-    sent(ac_recv, S_GC)
-    for k in range(P_CHUNKS):
+    sent(parts.at[pl.ds(0, 16)], S_GC)
+
+
+def hidden_grads(
+    losses, total, qb, pb, projection, losses_out, proj_out, gq_out, gp_hbm, gp, sem
+):
+    rows = gp.shape[0] // OUT_CHUNKS
+
+    def unload(k):
+        at = pl.ds(k * rows, rows)
+        return pltpu.make_async_copy(gp.at[at], gp_hbm.at[at], sem.at[k])
+
+    for k in range(OUT_CHUNKS):
+        at = pl.ds(k * rows, rows)
+        gp[at, :] = contract_last(pb[at, :], projection[...]).astype(BF16)
+        unload(k).start()
+    gq_out[...] = contract_last(qb[...], projection[...]).astype(BF16)
+    proj_out[...] = total[...]
+    for k in range(losses_out.shape[0]):
+        losses_out[k] = losses[k, 0]
+    for k in range(OUT_CHUNKS):
         unload(k).wait()
 
 
@@ -589,8 +614,8 @@
         pltpu.VMEM((passages, 128), F32),
         pltpu.VMEM((8, 128), F32),
         pltpu.VMEM((16, 8, 128), F32),
+        pltpu.VMEM((32, 128), F32),
         pltpu.VMEM((8, 128), F32),
-        pltpu.VMEM((16, 8, 128), F32),
         pltpu.VMEM((16, dim, q_rows), BF16),
         pltpu.VMEM((8, dim, q_rows), BF16),
         pltpu.VMEM((8, dim, q_rows), BF16),
@@ -599,30 +624,30 @@
         pltpu.VMEM((dim, q_rows), BF16),
         pltpu.VMEM((dim, q_rows), BF16),
         pltpu.VMEM((dim, p_rows), BF16),
-        pltpu.VMEM((p_rows, width), BF16),
         pltpu.VMEM((width, dim), F32),
-        pltpu.VMEM((half, dim), F32),
-        pltpu.VMEM((half, dim), F32),
-        pltpu.VMEM((4, quarter, dim), F32),
+        pltpu.VMEM((width, dim), BF16),
+        pltpu.VMEM((half, dim), BF16),
+        pltpu.VMEM((half, dim), BF16),
+        pltpu.VMEM((4, quarter, dim), BF16),
         pltpu.VMEM((quarter, dim), F32),
         pltpu.VMEM((4, piece, dim), F32),
-        pltpu.VMEM((piece, dim), F32),
-        pltpu.VMEM((8, piece, dim), F32),
-        pltpu.VMEM((width, dim), F32),
+        pltpu.VMEM((piece, dim), BF16),
+        pltpu.VMEM((8, piece, dim), BF16),
+        pltpu.VMEM((32, piece, dim), BF16),
         pltpu.SemaphoreType.DMA((SEND.total,)),
         pltpu.SemaphoreType.DMA((RECV.total,)),
         pltpu.SemaphoreType.DMA((LOCAL.total,)),
     ]
-    losses, grad_proj, grad_query, grad_passage = pl.pallas_call(
+    losses, grad_proj, query_back, passage_back = pl.pallas_call(
         kernel,
         out_shape=(
             jax.ShapeDtypeStruct((8, 128), F32),
             jax.ShapeDtypeStruct((width, dim), F32),
-            jax.ShapeDtypeStruct((q_rows, width), BF16),
-            jax.ShapeDtypeStruct((p_rows, width), BF16),
+            jax.ShapeDtypeStruct((q_rows, dim), BF16),
+            jax.ShapeDtypeStruct((p_rows, dim), BF16),
         ),
         in_specs=[smem, smem, vmem, hbm, vmem, vmem],
-        out_specs=(vmem, vmem, vmem, hbm),
+        out_specs=(vmem, vmem, vmem, vmem),
         scratch_shapes=scratch,
         compiler_params=pltpu.CompilerParams(
             collective_id=0, has_side_effects=True, vmem_limit_bytes=60 << 20
@@ -636,8 +661,25 @@
         projection,
         hard_ids,
     )
+    losses, grad_proj, grad_query, grad_passage = pl.pallas_call(
+        hidden_grads,
+        out_shape=(
+            jax.ShapeDtypeStruct((queries,), F32),
+            jax.ShapeDtypeStruct((width, dim), F32),
+            jax.ShapeDtypeStruct((q_rows, width), BF16),
+            jax.ShapeDtypeStruct((p_rows, width), BF16),
+        ),
+        in_specs=[smem, vmem, vmem, vmem, vmem],
+        out_specs=(smem, vmem, vmem, hbm),
+        scratch_shapes=[
+            pltpu.VMEM((p_rows, width), BF16),
+            pltpu.SemaphoreType.DMA((OUT_CHUNKS,)),
+        ],
+        compiler_params=pltpu.CompilerParams(vmem_limit_bytes=16 << 20),
+        name="hidden_grads",
+    )(losses, grad_proj, query_back, passage_back, projection)
     return (
-        losses[:, 0],
+        losses,
         grad_proj,
         grad_query.reshape(query_hidden.shape),
         grad_passage.reshape(passage_hidden.shape),

time: 92.8 us -> 88.5 us (0.954)
  local copies, waits for them, and re-layouts: 8.66 us -> 3.55 us
    unnamed x3 -> x10, local copies, waits for them, and re-layouts: 7.36 us -> 3.55 us
    pallas_call x0 -> x1, Pallas kernels: none -> 3.57 us  [local(): pl.pallas_call(hidden_grads, out_shape=(jax.ShapeDtypeStruct((queries,),...]
    pallas_call x1, Pallas kernels: 83.3 us -> 80.4 us  [local(): pl.pallas_call(kernel, out_shape=(jax.ShapeDtypeStruct((8, 128), F32), ja...]
    slice x1 -> x0, local copies, waits for them, and re-layouts: 1.3 us -> none  [local(): losses[:, 0]]
where the time goes in v2:
time: 88.5 us; the launch traced here: 88.2 us
  Pallas kernels  84 us (95%)
  local copies, waits for them, and re-layouts  3.55 us (4%)
    pallas_call x1, Pallas kernels, local(): pl.pallas_call(kernel, out_shape=(jax.ShapeDtypeStruct((8, 128), F32), ja...  80.4 us
    pallas_call x1, Pallas kernels, local(): pl.pallas_call(hidden_grads, out_shape=(jax.ShapeDtypeStruct((queries,),...  3.57 us
    unnamed x10, local copies, waits for them, and re-layouts  3.55 us

profile of v2, /device:TPU:1, one launch (start us, length us, event | category | flops | bytes accessed | tf_op | source)
XLA Modules:
  0.0 88.2 jit_solution(4834357788623911596)
XLA Ops:
  0.6 0.0 copy-start
  0.6 80.4 %late_interaction_step.1 = (f32[8,128]{1,0:T(8,128)}, f32[768,128]{1,0:T(8,128)}, bf16[256,128]{1,0:T(8,128)(2,1)}, bf16[2048,128]{1,0:T(8,128)(2,1)}) custom-call(s32[16]{0:T(128)} %plen.1, s32[8]{0:T(128)} %positive.1, bf16[256,768]{1,0:T(8,128)(2,1)} %bitcast.5, bf16[2048,768]{1,0:T(8,128)(2,1)} %bitcast.4, bf16[768,128]{1,0:T(8,128)(2,1)} %projection.3, ...), custom_call_target="tpu_custom_call" | custom-call | tf_op jit(solution)/shard_map/late_interaction_step/pallas_call | solution.py:641
  81.1 0.0 copy-done
  81.1 0.0 copy-start.1
  81.1 1.0 %copy-done.1 = bf16[2048,128]{1,0:T(8,128)(2,1)S(1)} copy-done((bf16[2048,128]{1,0:T(8,128)(2,1)S(1)}, bf16[2048,128]{1,0:T(8,128)(2,1)}, u32[]{:S(2)}) %copy-start.1) | copy-done | bytes 524312
  82.1 0.0 copy-start.2
  82.1 1.0 %copy-done.2 = f32[768,128]{1,0:T(8,128)S(1)} copy-done((f32[768,128]{1,0:T(8,128)S(1)}, f32[768,128]{1,0:T(8,128)}, u32[]{:S(2)}) %copy-start.2) | copy-done | bytes 393240
  83.1 0.0 copy-start.3
  83.1 0.8 copy-done.3
  84.0 0.0 copy-start.4
  84.0 0.7 copy-done.4
  84.7 3.6 %hidden_grads.1 = (f32[8]{0:T(128)}, f32[768,128]{1,0:T(8,128)}, bf16[256,768]{1,0:T(8,128)(2,1)}, bf16[2048,768]{1,0:T(8,128)(2,1)}) custom-call(f32[8,128]{1,0:T(8,128)S(1)} %copy-done.4, f32[768,128]{1,0:T(8,128)S(1)} %copy-done.2, bf16[256,128]{1,0:T(8,128)(2,1)S(1)} %copy-done.3, bf16[2048,128]{1,0:T(8,128)(2,1)S(1)} %copy-done.1, ...), custom_call_target="tpu_custom_call" | custom-call | tf_op jit(solution)/shard_map/hidden_grads/pallas_call | solution.py:664
Async XLA Ops:
  0.6 80.5 %copy-start = (bf16[768,128]{1,0:T(8,128)(2,1)S(1)}, bf16[768,128]{1,0:T(8,128)(2,1)}, u32[]{:S(2)}) copy-start(bf16[768,128]{1,0:T(8,128)(2,1)} %projection.3) | copy-start | bytes 589828
  81.1 1.0 %copy-start.1 = (bf16[2048,128]{1,0:T(8,128)(2,1)S(1)}, bf16[2048,128]{1,0:T(8,128)(2,1)}, u32[]{:S(2)}) copy-start(bf16[2048,128]{1,0:T(8,128)(2,1)} %get-tuple-element.15.pb) | copy-start | bytes 1572868
  82.1 1.0 %copy-start.2 = (f32[768,128]{1,0:T(8,128)S(1)}, f32[768,128]{1,0:T(8,128)}, u32[]{:S(2)}) copy-start(f32[768,128]{1,0:T(8,128)} %get-tuple-element.13.total) | copy-start | bytes 1179652
  83.1 0.8 copy-start.3
  84.0 0.7 copy-start.4

commit v3 on v2

--- a/solution.py
+++ b/solution.py
@@ -22,6 +22,10 @@
 GROUP_RELATIVE = [(dz, dx, dc) for dz in range(2) for dx in range(4) for dc in range(2)]
 
 PLANE_RELATIVE = [(dx, dc, dy) for dx in range(4) for dc in range(2) for dy in range(4)]
+
+PLANE_FAR_FIRST = sorted(
+    PLANE_RELATIVE[1:], key=lambda r: (-min(r[0], 4 - r[0]) - min(r[2], 4 - r[2]), r)
+)
 
 
 def slot_of(dz, dx, dc):
@@ -65,29 +69,29 @@
 S_QC, R_QC = SEND.take(8), RECV.take(8)
 S_QX, R_QX = SEND.take(8), RECV.take(8)
 S_QZ, R_QZ = SEND.take(1), RECV.take(1)
-S_AC, R_AC = SEND.take(1), RECV.take(1)
-S_AX, R_AX = SEND.take(4), RECV.take(4)
-S_AY, R_AY = SEND.take(4), RECV.take(4)
+S_RP, R_RP = SEND.take(32), RECV.take(32)
 S_AZ, R_AZ = SEND.take(8), RECV.take(8)
-S_GY, R_GY = SEND.take(4), RECV.take(4)
-S_GX, R_GX = SEND.take(4), RECV.take(4)
-S_GC, R_GC = SEND.take(1), RECV.take(1)
+S_GP, R_GP = SEND.take(32), RECV.take(32)
 P_CHUNKS = 4
-OUT_CHUNKS = 4
+OUT_CHUNKS = 8
 L_IN = LOCAL.take(P_CHUNKS)
+L_QUERY, L_PROJ, L_TOTAL = LOCAL.take(1), LOCAL.take(1), LOCAL.take(1)
+L_QB, L_PB = LOCAL.take(1), LOCAL.take(P_CHUNKS)
 
 
 def kernel(
     plen,
     positive,
-    query_hidden,
+    query_hbm,
     passage_hbm,
-    projection,
+    projection_hbm,
     hard_ids,
     losses_out,
-    fin,
-    qb_out,
-    pb_out,
+    total_hbm,
+    qb_hbm,
+    pb_hbm,
+    query_hidden,
+    projection,
     ph,
     q_pre,
     p_pre,
@@ -97,6 +101,7 @@
     qg,
     e_ref,
     sums,
+    spread_from,
     w_ref,
     pg,
     meta,
@@ -115,15 +120,13 @@
     rx,
     zs,
     rz,
+    pb_ref,
     pb_t,
+    qb_ref,
     w_loc,
     w_send,
-    ac_recv,
-    h_core,
-    ax_recv,
-    h_x,
-    ay_recv,
-    h_y,
+    rp_recv,
+    h_send,
     az_recv,
     parts,
     ssem,
@@ -192,6 +195,10 @@
         at = pl.ds(k * rows_in, rows_in)
         return pltpu.make_async_copy(passage_hbm.at[at], ph.at[at], lsem.at[L_IN + k])
 
+    load_query = pltpu.make_async_copy(query_hbm, query_hidden, lsem.at[L_QUERY])
+    load_proj = pltpu.make_async_copy(projection_hbm, projection, lsem.at[L_PROJ])
+    load_query.start()
+    load_proj.start()
     for k in range(P_CHUNKS):
         load(k).start()
 
@@ -202,6 +209,8 @@
     for peer in peers:
         pl.semaphore_signal(barrier, inc=1, device_id=peer, device_id_type=MESH)
 
+    load_query.wait()
+    load_proj.wait()
     pre = jnp.dot(query_hidden[...], projection[...], preferred_element_type=F32)
     q_pre[...] = pre
     scale = lax.rsqrt(jnp.sum(pre * pre, axis=-1, keepdims=True) + norm_eps)
@@ -290,6 +299,28 @@
                 e_ref[k, p * 128 : (p + 1) * 128, :] = live.astype(BF16)
                 sums[k, p : p + 1, :] = jnp.sum(live, axis=0, keepdims=True)
 
+    tokens = sums.shape[2]
+    spread_from[...] = (
+        lax.broadcasted_iota(jnp.int32, (tokens, 128), 0) // 32
+        == lax.rem(lax.broadcasted_iota(jnp.int32, (tokens, 128), 1), 8)
+    ).astype(F32)
+    lane_group = lax.broadcasted_iota(jnp.int32, (passages, 128), 1) // 8
+
+    def score(t):
+        pair = sums[pl.ds(2 * t, 2)].reshape(2 * passages, tokens)
+        part = jnp.dot(
+            0.1 * jnp.log(pair),
+            spread_from[...],
+            precision=HIGHEST,
+            preferred_element_type=F32,
+        )
+        first = group_of(t // 4, lax.rem(t, 4), 0)
+        second = group_of(t // 4, lax.rem(t, 4), 1)
+        score_ref[...] += jnp.where(lane_group == first, part[:passages], 0.0) + jnp.where(
+            lane_group == second, part[passages:], 0.0
+        )
+
+    score_ref[...] = jnp.zeros_like(score_ref)
     grow(0)
     relay_x(0, S_GATHER + 5)
     arrived(qg.at[1], R_GATHER + 1)
@@ -309,44 +340,30 @@
             relay_x(1, S_GATHER + 12)
 
         arrived(qg.at[2 * t + 1], R_GATHER + 2 * t + 1)
+        score(t - 1)
         grow(2 * t)
         grow(2 * t + 1)
         return carry
 
     lax.fori_loop(1, 8, forward, 0)
 
-    tokens = sums.shape[2]
-    every = sums[...].reshape(16 * passages, tokens)
-    spread_from = (
-        lax.broadcasted_iota(jnp.int32, (tokens, 128), 0) // 32
-        == lax.rem(lax.broadcasted_iota(jnp.int32, (tokens, 128), 1), 8)
-    ).astype(F32)
+    score(7)
+    scores = score_ref[...]
     spread_to = (
         lax.broadcasted_iota(jnp.int32, (128, tokens), 1) // 32
         == lax.rem(lax.broadcasted_iota(jnp.int32, (128, tokens), 0), 8)
     ).astype(F32)
-    per_slot = jnp.dot(
-        0.1 * jnp.log(every), spread_from, precision=HIGHEST, preferred_element_type=F32
-    )
-    lane_group = lax.broadcasted_iota(jnp.int32, (passages, 128), 1) // 8
-    scores = jnp.zeros((passages, 128), F32)
-    for dz, dx, dc in GROUP_RELATIVE:
-        slot = slot_of(dz, dx, dc)
-        part = per_slot[slot * passages : (slot + 1) * passages]
-        scores += jnp.where(lane_group == group_of(dz, dx, dc), part, 0.0)
-
     counts, chosen = counts_ref[...], chosen_ref[...]
     grown = jnp.exp(scores - SHIFT)
     hard = counts * grown
     other_hard = jnp.where(chosen > 0.5, 0.0, hard)
-    score_ref[...] = scores
     st_send[...] = jnp.zeros_like(st_send)
     st_send[0:1, :] = jnp.sum(grown, axis=0, keepdims=True)
     st_send[1:2, :] = jnp.sum(other_hard * grown, axis=0, keepdims=True)
     st_send[2:3, :] = jnp.sum(chosen * scores, axis=0, keepdims=True)
     h_recv[0:1, :] = jnp.sum(hard, axis=0, keepdims=True)
     own = h_recv.at[pl.ds(0, 1)]
-    for dx, dc, dy in PLANE_RELATIVE[1:]:
+    for dx, dc, dy in PLANE_FAR_FIRST:
         at = dx * 8 + dc * 4 + dy
         to = back(dx, 4) * 8 + dc * 4 + back(dy, 4)
         push(own, h_recv.at[pl.ds(to, 1)], S_HARD + at, R_HARD + to, in_plane(dx, dc, dy))
@@ -359,6 +376,8 @@
             R_STATS + to,
             in_group(dz, dx, dc),
         )
+    w_ref[...] = 1.0 / sums[...]
+    pg[...] = jnp.zeros_like(pg)
     for n in range(1, 32):
         arrived(h_recv.at[pl.ds(n, 1)], R_HARD + n)
     hz_recv[0:1, :] = jnp.sum(h_recv[...], axis=0, keepdims=True)
@@ -391,8 +410,7 @@
         precision=HIGHEST,
         preferred_element_type=F32,
     )
-    w_ref[...] = (spread / every).reshape(w_ref.shape)
-    pg[...] = jnp.zeros_like(pg)
+    w_ref[...] *= spread.reshape(w_ref.shape)
 
     def combine(j):
         arrived(rc.at[j], R_QC + j)
@@ -457,86 +475,60 @@
     lax.fori_loop(0, 16, backward, 0)
     combine(7)
 
+    def store_pb(k):
+        at = pl.ds(k * rows_in, rows_in)
+        return pltpu.make_async_copy(pb_ref.at[at], pb_hbm.at[at], lsem.at[L_PB + k])
+
+    store_qb = pltpu.make_async_copy(qb_ref, qb_hbm, lsem.at[L_QB])
+    store_total = pltpu.make_async_copy(parts, total_hbm, lsem.at[L_TOTAL])
+
     for k in range(P_CHUNKS):
         at = pl.ds(k * rows_in, rows_in)
         pb = norm_vjp(p_pre[at, :], pg[at, :]).astype(BF16)
         pb_t[:, at] = pb.T
-        pb_out[at, :] = pb
+        pb_ref[at, :] = pb
+        store_pb(k).start()
     w_t = jnp.dot(pb_t[...], ph[...], preferred_element_type=F32)
     w_loc[...] = w_t.T
 
     arrived(rz, R_QZ)
     whole = over_x(1) + rz[...].astype(F32)
     qb = norm_vjp(q_pre[...], whole.T).astype(BF16)
-    qb_out[...] = qb
+    qb_ref[...] = qb
     whole = w_loc[...] + jnp.dot(qh_t[...], qb, preferred_element_type=F32)
     w_loc[...] = whole
-    w_send[...] = whole.astype(BF16)
-
-    half = w_loc.shape[0] // 2
-    quarter = half // 4
-    piece = quarter // 4
-
-    def rows_at(first, count):
-        return pl.ds(pl.multiple_of(first, 8), count)
-
-    push(w_send.at[rows_at((1 - c) * half, half)], ac_recv, S_AC, R_AC, partner)
-    arrived(ac_recv, R_AC)
-    mine = w_loc[rows_at(c * half, half), :] + ac_recv[...].astype(F32)
-    w_loc[rows_at(c * half, half), :] = mine
-    h_core[...] = mine.astype(BF16)
-    for d in (2, 1, 3):
-        push(
-            h_core.at[rows_at(lax.rem(x + d, 4) * quarter, quarter)],
-            ax_recv.at[4 - d],
-            S_AX + d,
-            R_AX + 4 - d,
-            at_x(d),
-        )
-    base = c * half + x * quarter
-    mine = w_loc[rows_at(base, quarter), :]
-    for d in (1, 3, 2):
-        arrived(ax_recv.at[d], R_AX + d)
-        mine += ax_recv[d].astype(F32)
-    h_x[...] = mine
-    for d in (2, 1, 3):
-        push(
-            h_x.at[rows_at(lax.rem(y + d, 4) * piece, piece)],
-            ay_recv.at[4 - d],
-            S_AY + d,
-            R_AY + 4 - d,
-            at_y(d),
-        )
-    mine = h_x[rows_at(y * piece, piece), :]
-    for d in (1, 3, 2):
-        arrived(ay_recv.at[d], R_AY + d)
-        mine += ay_recv[d]
-    h_y[...] = mine.astype(BF16)
+
+    piece = h_send.shape[0]
+    for k in range(32):
+        w_send[k] = whole[k * piece : (k + 1) * piece].astype(BF16)
+    here = (c * 4 + x) * 4 + y
+    for dx, dc, dy in PLANE_FAR_FIRST:
+        at = dx * 8 + dc * 4 + dy
+        to = back(dx, 4) * 8 + dc * 4 + back(dy, 4)
+        there = (lax.rem(c + dc, 2) * 4 + lax.rem(x + dx, 4)) * 4 + lax.rem(y + dy, 4)
+        push(w_send.at[there], rp_recv.at[to], S_RP + at, R_RP + to, in_plane(dx, dc, dy))
+    store_qb.start()
+    mine = w_loc[pl.ds(pl.multiple_of(here * piece, 8), piece), :]
+    for n in range(1, 32):
+        arrived(rp_recv.at[n], R_RP + n)
+        mine += rp_recv[n].astype(F32)
+    h_send[...] = mine.astype(BF16)
     for d in (4, 3, 5, 2, 6, 1, 7):
-        push(h_y, az_recv.at[z], S_AZ + d, R_AZ + 8 - d, at_z(d))
-    az_recv[z] = h_y[...]
+        push(h_send, az_recv.at[z], S_AZ + d, R_AZ + 8 - d, at_z(d))
+    az_recv[z] = h_send[...]
     for d in range(1, 8):
         arrived(az_recv.at[0], R_AZ + d)
     mine = az_recv[0].astype(F32)
     for k in range(1, 8):
         mine += az_recv[k].astype(F32)
-    place = (c * 4 + x) * 4
-    parts[place + y] = mine.astype(BF16)
-    own = parts.at[place + y]
-    for d in (2, 1, 3):
-        push(own, own, S_GY + d, R_GY + 4 - d, at_y(d))
-    for d in range(1, 4):
-        arrived(own, R_GY + d)
-    own = parts.at[pl.ds(place, 4)]
-    for d in (2, 1, 3):
-        push(own, own, S_GX + d, R_GX + 4 - d, at_x(d))
-    for d in range(1, 4):
-        arrived(own, R_GX + d)
-    own = parts.at[pl.ds(c * 16, 16)]
-    push(own, own, S_GC, R_GC, partner)
-    arrived(own, R_GC)
-    for k in range(32):
-        fin[k * piece : (k + 1) * piece, :] = parts[k].astype(F32)
+    parts[here] = mine.astype(BF16)
+    for dx, dc, dy in PLANE_FAR_FIRST:
+        at = dx * 8 + dc * 4 + dy
+        to = back(dx, 4) * 8 + dc * 4 + back(dy, 4)
+        push(parts.at[here], parts.at[here], S_GP + at, R_GP + to, in_plane(dx, dc, dy))
+    for n in range(1, 32):
+        arrived(parts.at[0], R_GP + n)
+    store_total.start()
 
     for n in range(15):
         sent(qg.at[0], S_GATHER + n)
@@ -552,36 +544,80 @@
         if n % 4 != 3:
             sent(cs.at[0], S_QX + n)
     sent(zs, S_QZ)
-    sent(ac_recv, S_AC)
-    for d in range(1, 4):
-        sent(ax_recv.at[0], S_AX + d)
-        sent(ay_recv.at[0], S_AY + d)
-        sent(parts.at[0], S_GY + d)
-        sent(parts.at[pl.ds(0, 4)], S_GX + d)
+    for n in range(1, 32):
+        sent(w_send.at[0], S_RP + n)
+        sent(parts.at[0], S_GP + n)
     for d in range(1, 8):
-        sent(h_y, S_AZ + d)
-    sent(parts.at[pl.ds(0, 16)], S_GC)
+        sent(h_send, S_AZ + d)
+    store_qb.wait()
+    for k in range(P_CHUNKS):
+        store_pb(k).wait()
+    store_total.wait()
 
 
 def hidden_grads(
-    losses, total, qb, pb, projection, losses_out, proj_out, gq_out, gp_hbm, gp, sem
+    losses_hbm,
+    total_hbm,
+    qb_hbm,
+    pb_hbm,
+    projection_hbm,
+    losses_out,
+    proj_hbm,
+    gq_hbm,
+    gp_hbm,
+    losses,
+    total,
+    qb,
+    pb,
+    projection,
+    proj,
+    gq,
+    gp,
+    sem,
 ):
     rows = gp.shape[0] // OUT_CHUNKS
+    loads = [
+        pltpu.make_async_copy(src, dst, sem.at[n])
+        for n, (src, dst) in enumerate(
+            (
+                (projection_hbm, projection),
+                (pb_hbm, pb),
+                (qb_hbm, qb),
+                (total_hbm, total),
+                (losses_hbm, losses),
+            )
+        )
+    ]
 
     def unload(k):
         at = pl.ds(k * rows, rows)
-        return pltpu.make_async_copy(gp.at[at], gp_hbm.at[at], sem.at[k])
-
+        return pltpu.make_async_copy(gp.at[at], gp_hbm.at[at], sem.at[5 + k])
+
+    store_proj = pltpu.make_async_copy(proj, proj_hbm, sem.at[5 + OUT_CHUNKS])
+    store_gq = pltpu.make_async_copy(gq, gq_hbm, sem.at[6 + OUT_CHUNKS])
+    for copy in loads:
+        copy.start()
+    loads[0].wait()
+    loads[1].wait()
     for k in range(OUT_CHUNKS):
         at = pl.ds(k * rows, rows)
         gp[at, :] = contract_last(pb[at, :], projection[...]).astype(BF16)
         unload(k).start()
-    gq_out[...] = contract_last(qb[...], projection[...]).astype(BF16)
-    proj_out[...] = total[...]
+    loads[2].wait()
+    gq[...] = contract_last(qb[...], projection[...]).astype(BF16)
+    store_gq.start()
+    loads[3].wait()
+    piece = total.shape[1]
+    for k in range(total.shape[0]):
+        proj[k * piece : (k + 1) * piece, :] = total[k].astype(F32)
+    store_proj.start()
+    loads[4].wait()
     for k in range(losses_out.shape[0]):
         losses_out[k] = losses[k, 0]
     for k in range(OUT_CHUNKS):
         unload(k).wait()
+    store_gq.wait()
+    store_proj.wait()
 
 
 def local(query_hidden, passage_hidden, projection, positive, hard_ids, passage_len):
@@ -589,13 +625,13 @@
     passages, slots, _ = passage_hidden.shape
     dim = projection.shape[1]
     q_rows, p_rows = queries * query_len, passages * slots
-    half = width // 2
-    quarter = half // 4
-    piece = quarter // 4
+    piece = width // 32
     vmem = pl.BlockSpec(memory_space=pltpu.VMEM)
     smem = pl.BlockSpec(memory_space=pltpu.SMEM)
     hbm = pl.BlockSpec(memory_space=pl.ANY)
     scratch = [
+        pltpu.VMEM((q_rows, width), BF16),
+        pltpu.VMEM((width, dim), BF16),
         pltpu.VMEM((p_rows, width), BF16),
         pltpu.VMEM((q_rows, dim), F32),
         pltpu.VMEM((p_rows, dim), F32),
@@ -605,6 +641,7 @@
         pltpu.VMEM((16, q_rows, dim), BF16),
         pltpu.VMEM((16, p_rows, q_rows), BF16),
         pltpu.VMEM((16, passages, q_rows), F32),
+        pltpu.VMEM((q_rows, 128), F32),
         pltpu.VMEM((16, passages, q_rows), F32),
         pltpu.VMEM((p_rows, dim), F32),
         pltpu.VMEM((16, 8, 128), F32),
@@ -623,14 +660,12 @@
         pltpu.VMEM((8, dim, q_rows), BF16),
         pltpu.VMEM((dim, q_rows), BF16),
         pltpu.VMEM((dim, q_rows), BF16),
+        pltpu.VMEM((p_rows, dim), BF16),
         pltpu.VMEM((dim, p_rows), BF16),
+        pltpu.VMEM((q_rows, dim), BF16),
         pltpu.VMEM((width, dim), F32),
-        pltpu.VMEM((width, dim), BF16),
-        pltpu.VMEM((half, dim), BF16),
-        pltpu.VMEM((half, dim), BF16),
-        pltpu.VMEM((4, quarter, dim), BF16),
-        pltpu.VMEM((quarter, dim), F32),
-        pltpu.VMEM((4, piece, dim), F32),
+        pltpu.VMEM((32, piece, dim), BF16),
+        pltpu.VMEM((32, piece, dim), BF16),
         pltpu.VMEM((piece, dim), BF16),
         pltpu.VMEM((8, piece, dim), BF16),
         pltpu.VMEM((32, piece, dim), BF16),
@@ -638,16 +673,16 @@
         pltpu.SemaphoreType.DMA((RECV.total,)),
         pltpu.SemaphoreType.DMA((LOCAL.total,)),
     ]
-    losses, grad_proj, query_back, passage_back = pl.pallas_call(
+    losses, total, query_back, passage_back = pl.pallas_call(
         kernel,
         out_shape=(
             jax.ShapeDtypeStruct((8, 128), F32),
-            jax.ShapeDtypeStruct((width, dim), F32),
+            jax.ShapeDtypeStruct((32, piece, dim), BF16),
             jax.ShapeDtypeStruct((q_rows, dim), BF16),
             jax.ShapeDtypeStruct((p_rows, dim), BF16),
         ),
-        in_specs=[smem, smem, vmem, hbm, vmem, vmem],
-        out_specs=(vmem, vmem, vmem, vmem),
+        in_specs=[smem, smem, hbm, hbm, hbm, vmem],
+        out_specs=(vmem, hbm, hbm, hbm),
         scratch_shapes=scratch,
         compiler_params=pltpu.CompilerParams(
             collective_id=0, has_side_effects=True, vmem_limit_bytes=60 << 20
@@ -669,15 +704,22 @@
             jax.ShapeDtypeStruct((q_rows, width), BF16),
             jax.ShapeDtypeStruct((p_rows, width), BF16),
         ),
-        in_specs=[smem, vmem, vmem, vmem, vmem],
-        out_specs=(smem, vmem, vmem, hbm),
+        in_specs=[hbm] * 5,
+        out_specs=(smem, hbm, hbm, hbm),
         scratch_shapes=[
+            pltpu.SMEM((8, 128), F32),
+            pltpu.VMEM((32, piece, dim), BF16),
+            pltpu.VMEM((q_rows, dim), BF16),
+            pltpu.VMEM((p_rows, dim), BF16),
+            pltpu.VMEM((width, dim), BF16),
+            pltpu.VMEM((width, dim), F32),
+            pltpu.VMEM((q_rows, width), BF16),
             pltpu.VMEM((p_rows, width), BF16),
-            pltpu.SemaphoreType.DMA((OUT_CHUNKS,)),
+            pltpu.SemaphoreType.DMA((7 + OUT_CHUNKS,)),
         ],
-        compiler_params=pltpu.CompilerParams(vmem_limit_bytes=16 << 20),
+        compiler_params=pltpu.CompilerParams(vmem_limit_bytes=60 << 20),
         name="hidden_grads",
-    )(losses, grad_proj, query_back, passage_back, projection)
+    )(losses, total, query_back, passage_back, projection)
     return (
         losses,
         grad_proj,

time: 88.5 us -> 79 us (0.89)
  Pallas kernels: 84 us -> 78.2 us
  local copies, waits for them, and re-layouts: 3.55 us -> 0 us
    pallas_call x1, Pallas kernels: 80.4 us -> 74.2 us  [local(): pl.pallas_call(kernel, out_shape=(jax.ShapeDtypeStruct((8, 128), F32), ja...]
    unnamed x10 -> x0, local copies, waits for them, and re-layouts: 3.55 us -> none
where the time goes in v3:
time: 79 us; the launch traced here: 78.8 us
  Pallas kernels  78.2 us (99%)
    pallas_call x1, Pallas kernels, local(): pl.pallas_call(kernel, out_shape=(jax.ShapeDtypeStruct((8, 128), F32), ja...  74.2 us
    pallas_call x1, Pallas kernels, local(): pl.pallas_call(hidden_grads, out_shape=(jax.ShapeDtypeStruct((queries,),...  3.99 us

profile of v3, /device:TPU:1, one launch (start us, length us, event | category | flops | bytes accessed | tf_op | source)
XLA Modules:
  0.0 78.8 jit_solution(5146036169811827346)
XLA Ops:
  0.6 74.2 %late_interaction_step.1 = (f32[8,128]{1,0:T(8,128)}, bf16[32,24,128]{2,1,0:T(8,128)(2,1)}, bf16[256,128]{1,0:T(8,128)(2,1)}, bf16[2048,128]{1,0:T(8,128)(2,1)}) custom-call(s32[16]{0:T(128)} %plen.1, s32[8]{0:T(128)} %positive.1, bf16[256,768]{1,0:T(8,128)(2,1)} %bitcast.5, bf16[2048,768]{1,0:T(8,128)(2,1)} %bitcast.4, bf16[768,128]{1,0:T(8,128)(2,1)} %projection_hbm.3, ...), custom_call_target="tpu_custom_call" | custom-call | tf_op jit(solution)/shard_map/late_interaction_step/pallas_call | solution.py:676
  74.9 4.0 %hidden_grads.1 = (f32[8]{0:T(128)}, f32[768,128]{1,0:T(8,128)}, bf16[256,768]{1,0:T(8,128)(2,1)}, bf16[2048,768]{1,0:T(8,128)(2,1)}) custom-call(f32[8,128]{1,0:T(8,128)} %get-tuple-element.12.losses_hbm, bf16[32,24,128]{2,1,0:T(8,128)(2,1)} %get-tuple-element.13.total_hbm, bf16[256,128]{1,0:T(8,128)(2,1)} %get-tuple-element.14.qb_hbm, ...), custom_call_target="tpu_custom_call" | custom-call | tf_op jit(solution)/shard_map/hidden_grads/pallas_call | solution.py:699

commit v4 on v3

--- a/solution.py
+++ b/solution.py
@@ -73,10 +73,11 @@
 S_AZ, R_AZ = SEND.take(8), RECV.take(8)
 S_GP, R_GP = SEND.take(32), RECV.take(32)
 P_CHUNKS = 4
+FSTEP = 4
+BSTEP = 4
 OUT_CHUNKS = 8
 L_IN = LOCAL.take(P_CHUNKS)
-L_QUERY, L_PROJ, L_TOTAL = LOCAL.take(1), LOCAL.take(1), LOCAL.take(1)
-L_QB, L_PB = LOCAL.take(1), LOCAL.take(P_CHUNKS)
+L_QUERY, L_PROJ = LOCAL.take(1), LOCAL.take(1)
 
 
 def kernel(
@@ -87,9 +88,9 @@
     projection_hbm,
     hard_ids,
     losses_out,
-    total_hbm,
-    qb_hbm,
-    pb_hbm,
+    total_out,
+    gq_out,
+    gp_out,
     query_hidden,
     projection,
     ph,
@@ -102,6 +103,7 @@
     e_ref,
     sums,
     spread_from,
+    one_lane,
     w_ref,
     pg,
     meta,
@@ -241,6 +243,12 @@
             in_group(dz, dx, dc),
         )
 
+    first_lane = lax.broadcasted_iota(jnp.int32, (128, 128), 1) == 0
+    token = lax.broadcasted_iota(jnp.int32, (128, 128), 0)
+    for p in range(plen.shape[0]):
+        padding = first_lane & (token >= plen[p])
+        pe[p * 128 : (p + 1) * 128, 128:256] = jnp.where(padding, -100.0, 0.0).astype(BF16)
+    one_lane[...] = (lax.broadcasted_iota(jnp.int32, one_lane.shape, 1) == 0).astype(BF16)
     for k in range(P_CHUNKS):
         load(k).wait()
         at = pl.ds(k * rows_in, rows_in)
@@ -248,7 +256,7 @@
         p_pre[at, :] = pre
         scale = lax.rsqrt(jnp.sum(pre * pre, axis=-1, keepdims=True) + norm_eps)
         unit = (pre * scale).astype(BF16)
-        pe[at, :] = unit
+        pe[at, 0:128] = unit
         pe_t[:, at] = unit.T
     qh_t[...] = query_hidden[...].T
 
@@ -284,18 +292,17 @@
         chosen_ref[...] = (turned[32:33, :] == own).astype(F32)
 
     passages = sums.shape[1]
-    step = 4
+    step = FSTEP
     height = step * 128
 
     def grow(k):
-        block = qg[k]
+        block = jnp.concatenate([qg[k], one_lane[...]], axis=1)
         for n in range(passages // step):
             similar = contract_last(pe[n * height : (n + 1) * height, :], block)
             grown = jnp.exp2(similar * EXP2_SCALE)
             for i in range(step):
                 p = n * step + i
-                token = lax.broadcasted_iota(jnp.int32, (128, grown.shape[1]), 0)
-                live = jnp.where(token < plen[p], grown[i * 128 : (i + 1) * 128], 0.0)
+                live = grown[i * 128 : (i + 1) * 128]
                 e_ref[k, p * 128 : (p + 1) * 128, :] = live.astype(BF16)
                 sums[k, p : p + 1, :] = jnp.sum(live, axis=0, keepdims=True)
 
@@ -435,59 +442,51 @@
             whole += rx[side * 4 + d].astype(F32)
         return whole
 
-    def backward(it, carry):
-        j = it // 2
+    def backward(j, carry):
         dz = 1 - j // 4
-        dx = lax.rem(j + 1, 4)
-        dc = 1 - lax.rem(it, 2)
-        k = dz * 8 + dx * 2 + dc
-        block = qg[k]
+        k = dz * 8 + lax.rem(j + 1, 4) * 2
+        both = qg[pl.ds(k, 2)].reshape(2 * tokens, qg.shape[2])
         acc = None
-        for n in range(passages // step):
+        for n in range(passages // BSTEP):
             parts = []
-            for i in range(step):
-                p = n * step + i
-                weight = w_ref[k, p : p + 1, :]
-                kept = e_ref[k, p * 128 : (p + 1) * 128, :].astype(F32)
-                parts.append((kept * weight).astype(BF16))
-            coefficient = jnp.concatenate(parts, axis=0)
-            at = slice(n * height, (n + 1) * height)
-            pg[at, :] += jnp.dot(coefficient, block, preferred_element_type=F32)
+            for i in range(BSTEP):
+                p = n * BSTEP + i
+                pair = [
+                    (
+                        e_ref[k + m, p * 128 : (p + 1) * 128, :].astype(F32)
+                        * w_ref[k + m, p : p + 1, :]
+                    ).astype(BF16)
+                    for m in range(2)
+                ]
+                parts.append(jnp.concatenate(pair, axis=1))
+            coefficient = jnp.concatenate(parts, axis=0) if BSTEP > 1 else parts[0]
+            at = slice(n * BSTEP * 128, (n + 1) * BSTEP * 128)
+            pg[at, :] += jnp.dot(coefficient, both, preferred_element_type=F32)
             term = jnp.dot(pe_t[:, at], coefficient, preferred_element_type=F32)
             acc = term if acc is None else acc + term
-        qgt[it] = acc.astype(BF16)
-
-        @pl.when(dc == 1)
+        qgt[2 * j] = acc[:, tokens:].astype(BF16)
+        push(qgt.at[2 * j], rc.at[j], S_QC + j, R_QC + j, partner)
+        qgt[2 * j + 1] = acc[:, :tokens].astype(BF16)
+
+        @pl.when(j >= 1)
         def _():
-            push(qgt.at[it], rc.at[j], S_QC + j, R_QC + j, partner)
-
-            @pl.when(it >= 2)
-            def _():
-                combine(j - 1)
-
-        @pl.when(it == 13)
+            combine(j - 1)
+
+        @pl.when(j == 6)
         def _():
             zs[...] = over_x(0).astype(BF16)
             push(zs, rz, S_QZ, R_QZ, across)
 
         return carry
 
-    lax.fori_loop(0, 16, backward, 0)
+    lax.fori_loop(0, 8, backward, 0)
     combine(7)
-
-    def store_pb(k):
-        at = pl.ds(k * rows_in, rows_in)
-        return pltpu.make_async_copy(pb_ref.at[at], pb_hbm.at[at], lsem.at[L_PB + k])
-
-    store_qb = pltpu.make_async_copy(qb_ref, qb_hbm, lsem.at[L_QB])
-    store_total = pltpu.make_async_copy(parts, total_hbm, lsem.at[L_TOTAL])
 
     for k in range(P_CHUNKS):
         at = pl.ds(k * rows_in, rows_in)
         pb = norm_vjp(p_pre[at, :], pg[at, :]).astype(BF16)
         pb_t[:, at] = pb.T
         pb_ref[at, :] = pb
-        store_pb(k).start()
     w_t = jnp.dot(pb_t[...], ph[...], preferred_element_type=F32)
     w_loc[...] = w_t.T
 
@@ -507,7 +506,10 @@
         to = back(dx, 4) * 8 + dc * 4 + back(dy, 4)
         there = (lax.rem(c + dc, 2) * 4 + lax.rem(x + dx, 4)) * 4 + lax.rem(y + dy, 4)
         push(w_send.at[there], rp_recv.at[to], S_RP + at, R_RP + to, in_plane(dx, dc, dy))
-    store_qb.start()
+    gq_out[...] = contract_last(qb_ref[...], projection[...]).astype(BF16)
+    for k in range(P_CHUNKS):
+        at = pl.ds(k * rows_in, rows_in)
+        gp_out[at, :] = contract_last(pb_ref[at, :], projection[...]).astype(BF16)
     mine = w_loc[pl.ds(pl.multiple_of(here * piece, 8), piece), :]
     for n in range(1, 32):
         arrived(rp_recv.at[n], R_RP + n)
@@ -528,7 +530,9 @@
         push(parts.at[here], parts.at[here], S_GP + at, R_GP + to, in_plane(dx, dc, dy))
     for n in range(1, 32):
         arrived(parts.at[0], R_GP + n)
-    store_total.start()
+    piece = total_out.shape[0] // 32
+    for k in range(32):
+        total_out[k * piece : (k + 1) * piece, :] = parts[k].astype(F32)
 
     for n in range(15):
         sent(qg.at[0], S_GATHER + n)
@@ -549,75 +553,22 @@
         sent(parts.at[0], S_GP + n)
     for d in range(1, 8):
         sent(h_send, S_AZ + d)
-    store_qb.wait()
-    for k in range(P_CHUNKS):
-        store_pb(k).wait()
-    store_total.wait()
-
-
-def hidden_grads(
-    losses_hbm,
-    total_hbm,
-    qb_hbm,
-    pb_hbm,
-    projection_hbm,
-    losses_out,
-    proj_hbm,
-    gq_hbm,
-    gp_hbm,
-    losses,
-    total,
-    qb,
-    pb,
-    projection,
-    proj,
-    gq,
-    gp,
-    sem,
-):
+
+
+def write_out(losses, total, gq, gp, losses_out, total_hbm, gq_hbm, gp_hbm, sem):
     rows = gp.shape[0] // OUT_CHUNKS
-    loads = [
-        pltpu.make_async_copy(src, dst, sem.at[n])
-        for n, (src, dst) in enumerate(
-            (
-                (projection_hbm, projection),
-                (pb_hbm, pb),
-                (qb_hbm, qb),
-                (total_hbm, total),
-                (losses_hbm, losses),
-            )
-        )
-    ]
-
-    def unload(k):
-        at = pl.ds(k * rows, rows)
-        return pltpu.make_async_copy(gp.at[at], gp_hbm.at[at], sem.at[5 + k])
-
-    store_proj = pltpu.make_async_copy(proj, proj_hbm, sem.at[5 + OUT_CHUNKS])
-    store_gq = pltpu.make_async_copy(gq, gq_hbm, sem.at[6 + OUT_CHUNKS])
-    for copy in loads:
-        copy.start()
-    loads[0].wait()
-    loads[1].wait()
+    copies = []
     for k in range(OUT_CHUNKS):
         at = pl.ds(k * rows, rows)
-        gp[at, :] = contract_last(pb[at, :], projection[...]).astype(BF16)
-        unload(k).start()
-    loads[2].wait()
-    gq[...] = contract_last(qb[...], projection[...]).astype(BF16)
-    store_gq.start()
-    loads[3].wait()
-    piece = total.shape[1]
-    for k in range(total.shape[0]):
-        proj[k * piece : (k + 1) * piece, :] = total[k].astype(F32)
-    store_proj.start()
-    loads[4].wait()
+        copies.append((gp.at[at], gp_hbm.at[at]))
+    copies += [(gq, gq_hbm), (total, total_hbm)]
+    copies = [pltpu.make_async_copy(a, b, sem.at[n]) for n, (a, b) in enumerate(copies)]
+    for copy in copies:
+        copy.start()
     for k in range(losses_out.shape[0]):
-        losses_out[k] = losses[k, 0]
-    for k in range(OUT_CHUNKS):
-        unload(k).wait()
-    store_gq.wait()
-    store_proj.wait()
+        losses_out[k] = jnp.sum(losses[k : k + 1, 0:1])
+    for copy in copies:
+        copy.wait()
 
 
 def local(query_hidden, passage_hidden, projection, positive, hard_ids, passage_len):
@@ -635,13 +586,14 @@
         pltpu.VMEM((p_rows, width), BF16),
         pltpu.VMEM((q_rows, dim), F32),
         pltpu.VMEM((p_rows, dim), F32),
-        pltpu.VMEM((p_rows, dim), BF16),
+        pltpu.VMEM((p_rows, 2 * dim), BF16),
         pltpu.VMEM((dim, p_rows), BF16),
         pltpu.VMEM((width, q_rows), BF16),
         pltpu.VMEM((16, q_rows, dim), BF16),
         pltpu.VMEM((16, p_rows, q_rows), BF16),
         pltpu.VMEM((16, passages, q_rows), F32),
         pltpu.VMEM((q_rows, 128), F32),
+        pltpu.VMEM((q_rows, 128), BF16),
         pltpu.VMEM((16, passages, q_rows), F32),
         pltpu.VMEM((p_rows, dim), F32),
         pltpu.VMEM((16, 8, 128), F32),
@@ -673,16 +625,16 @@
         pltpu.SemaphoreType.DMA((RECV.total,)),
         pltpu.SemaphoreType.DMA((LOCAL.total,)),
     ]
-    losses, total, query_back, passage_back = pl.pallas_call(
+    losses, total, query_grad, passage_grad = pl.pallas_call(
         kernel,
         out_shape=(
-            jax.ShapeDtypeStruct((8, 128), F32),
-            jax.ShapeDtypeStruct((32, piece, dim), BF16),
-            jax.ShapeDtypeStruct((q_rows, dim), BF16),
-            jax.ShapeDtypeStruct((p_rows, dim), BF16),
+            pltpu.VMEM((8, 128), F32),
+            pltpu.VMEM((width, dim), F32),
+            pltpu.VMEM((q_rows, width), BF16),
+            pltpu.VMEM((p_rows, width), BF16),
         ),
         in_specs=[smem, smem, hbm, hbm, hbm, vmem],
-        out_specs=(vmem, hbm, hbm, hbm),
+        out_specs=(vmem, vmem, vmem, vmem),
         scratch_shapes=scratch,
         compiler_params=pltpu.CompilerParams(
             collective_id=0, has_side_effects=True, vmem_limit_bytes=60 << 20
@@ -697,29 +649,19 @@
         hard_ids,
     )
     losses, grad_proj, grad_query, grad_passage = pl.pallas_call(
-        hidden_grads,
+        write_out,
         out_shape=(
             jax.ShapeDtypeStruct((queries,), F32),
             jax.ShapeDtypeStruct((width, dim), F32),
             jax.ShapeDtypeStruct((q_rows, width), BF16),
             jax.ShapeDtypeStruct((p_rows, width), BF16),
         ),
-        in_specs=[hbm] * 5,
+        in_specs=[vmem] * 4,
         out_specs=(smem, hbm, hbm, hbm),
-        scratch_shapes=[
-            pltpu.SMEM((8, 128), F32),
-            pltpu.VMEM((32, piece, dim), BF16),
-            pltpu.VMEM((q_rows, dim), BF16),
-            pltpu.VMEM((p_rows, dim), BF16),
-            pltpu.VMEM((width, dim), BF16),
-            pltpu.VMEM((width, dim), F32),
-            pltpu.VMEM((q_rows, width), BF16),
-            pltpu.VMEM((p_rows, width), BF16),
-            pltpu.SemaphoreType.DMA((7 + OUT_CHUNKS,)),
-        ],
-        compiler_params=pltpu.CompilerParams(vmem_limit_bytes=60 << 20),
-        name="hidden_grads",
-    )(losses, total, query_back, passage_back, projection)
+        scratch_shapes=[pltpu.SemaphoreType.DMA((2 + OUT_CHUNKS,))],
+        compiler_params=pltpu.CompilerParams(vmem_limit_bytes=1 << 20),
+        name="write_out",
+    )(losses, total, query_grad, passage_grad)
     return (
         losses,
         grad_proj,

time: 79 us -> 74.7 us (0.946)
  Pallas kernels: 78.2 us -> 74 us
    pallas_call x2, Pallas kernels: 78.2 us -> 74 us  [the longest x1 71.4 us: local(): pl.pallas_call(kernel, out_shape=(pltpu.VMEM((8, 128), F32), pltpu.VMEM((...]
where the time goes in v4:
time: 74.7 us; the launch traced here: 74.6 us
  Pallas kernels  74 us (99%)
    pallas_call x1, Pallas kernels, local(): pl.pallas_call(kernel, out_shape=(pltpu.VMEM((8, 128), F32), pltpu.VMEM((...  71.4 us
    pallas_call x1, Pallas kernels, local(): pl.pallas_call(write_out, out_shape=(jax.ShapeDtypeStruct((queries,), F32...  2.52 us

profile of v4, /device:TPU:1, one launch (start us, length us, event | category | flops | bytes accessed | tf_op | source)
XLA Modules:
  0.0 74.6 jit_solution(4410670086082683082)
XLA Ops:
  0.6 71.4 %late_interaction_step.1 = (f32[8,128]{1,0:T(8,128)S(1)}, f32[768,128]{1,0:T(8,128)S(1)}, bf16[256,768]{1,0:T(8,128)(2,1)S(1)}, bf16[2048,768]{1,0:T(8,128)(2,1)S(1)}) custom-call(s32[16]{0:T(128)} %plen.1, s32[8]{0:T(128)} %positive.1, bf16[256,768]{1,0:T(8,128)(2,1)} %bitcast.5, bf16[2048,768]{1,0:T(8,128)(2,1)} %bitcast.4, ...), custom_call_target="tpu_custom_call" | custom-call | tf_op jit(solution)/shard_map/late_interaction_step/pallas_call | solution.py:628
  72.1 2.5 %write_out.1 = (f32[8]{0:T(128)}, f32[768,128]{1,0:T(8,128)}, bf16[256,768]{1,0:T(8,128)(2,1)}, bf16[2048,768]{1,0:T(8,128)(2,1)}) custom-call(f32[8,128]{1,0:T(8,128)S(1)} %get-tuple-element.12.losses, f32[768,128]{1,0:T(8,128)S(1)} %get-tuple-element.13.total, bf16[256,768]{1,0:T(8,128)(2,1)S(1)} %get-tuple-element.14.gq, ...), custom_call_target="tpu_custom_call" | custom-call | tf_op jit(solution)/shard_map/write_out/pallas_call | solution.py:651

commit v5 on v4

--- a/solution.py
+++ b/solution.py
@@ -61,8 +61,8 @@
 SEND = Sems()
 RECV = Sems()
 LOCAL = Sems()
-S_GATHER, R_GATHER = SEND.take(15), RECV.take(16)
-S_META, R_META = SEND.take(16), RECV.take(16)
+S_GATHER, R_GATHER = SEND.take(11), RECV.take(16)
+S_HALF, R_HALF = SEND.take(8), RECV.take(32)
 S_STATS, R_STATS = SEND.take(16), RECV.take(16)
 S_HARD, R_HARD = SEND.take(32), RECV.take(32)
 S_HZ, R_HZ = SEND.take(8), RECV.take(8)
@@ -77,20 +77,23 @@
 BSTEP = 4
 OUT_CHUNKS = 8
 L_IN = LOCAL.take(P_CHUNKS)
-L_QUERY, L_PROJ = LOCAL.take(1), LOCAL.take(1)
+L_QUERY, L_PROJ, L_SMALL = LOCAL.take(1), LOCAL.take(1), LOCAL.take(3)
 
 
 def kernel(
-    plen,
-    positive,
+    plen_hbm,
+    positive_hbm,
     query_hbm,
     passage_hbm,
     projection_hbm,
-    hard_ids,
+    hard_ids_hbm,
     losses_out,
     total_out,
     gq_out,
     gp_out,
+    plen,
+    positive,
+    hard_ids,
     query_hidden,
     projection,
     ph,
@@ -134,6 +137,7 @@
     ssem,
     rsem,
     lsem,
+    entry,
 ):
     zh, x, c = lax.axis_index("zh"), lax.axis_index("x"), lax.axis_index("c")
     zl, y = lax.axis_index("zl"), lax.axis_index("y")
@@ -199,15 +203,24 @@
 
     load_query = pltpu.make_async_copy(query_hbm, query_hidden, lsem.at[L_QUERY])
     load_proj = pltpu.make_async_copy(projection_hbm, projection, lsem.at[L_PROJ])
+    small = [
+        pltpu.make_async_copy(src, dst, lsem.at[L_SMALL + n])
+        for n, (src, dst) in enumerate(
+            ((plen_hbm, plen), (positive_hbm, positive), (hard_ids_hbm, hard_ids))
+        )
+    ]
     load_query.start()
     load_proj.start()
+    for copy in small:
+        copy.start()
     for k in range(P_CHUNKS):
         load(k).start()
 
     barrier = pltpu.get_barrier_semaphore()
-    peers = [in_group(*r) for r in GROUP_RELATIVE[1:]]
-    peers += [in_plane(*r) for r in PLANE_RELATIVE[1:] if r[2]]
-    peers += [at_z(d) for d in range(1, 8) if d != 4]
+    peers = [partner]
+    peers += [at_x(d) for d in range(1, 4)]
+    peers += [at_y(d) for d in range(1, 4)]
+    peers += [at_z(d) for d in range(1, 8)]
     for peer in peers:
         pl.semaphore_signal(barrier, inc=1, device_id=peer, device_id_type=MESH)
 
@@ -216,33 +229,34 @@
     pre = jnp.dot(query_hidden[...], projection[...], preferred_element_type=F32)
     q_pre[...] = pre
     scale = lax.rsqrt(jnp.sum(pre * pre, axis=-1, keepdims=True) + norm_eps)
-    qg[0] = (pre * scale).astype(BF16)
+    qg[0, 0:256] = (pre * scale).astype(BF16)
 
     lanes = lax.broadcasted_iota(jnp.int32, (8, 128), 1)
     rows = lax.broadcasted_iota(jnp.int32, (8, 128), 0)
+    for copy in small:
+        copy.wait()
     chosen_row = jnp.zeros((8, 128), F32)
     for k in range(8):
         chosen_row = jnp.where(rows == k, positive[k].astype(F32), chosen_row)
-    meta[0] = jnp.where(lanes == 32, chosen_row, 0.0)
-    meta[0, :, 0:32] = hard_ids[...].astype(F32)
+    meta[0:8, :] = jnp.where(lanes == 32, chosen_row, 0.0)
+    meta[8:16, :] = jnp.zeros((8, 128), F32)
+    meta[0:8, 0:32] = hard_ids[...].astype(F32)
+    qg[0, 256:272] = meta[...].astype(BF16)
 
     pl.semaphore_wait(barrier, len(peers))
-
-    push(qg.at[0], qg.at[slot_of(1, 0, 0)], S_GATHER, R_GATHER + slot_of(1, 0, 0), across)
+    for d in range(1, 4):
+        pl.semaphore_signal(entry.at[0], inc=1, device_id=at_x(d), device_id_type=MESH)
+
+    def half_of(slot, h):
+        return qg.at[slot, pl.ds(h * 128, 144 if h else 128)]
+
+    far = slot_of(1, 0, 0)
+    for h in range(2):
+        push(half_of(0, h), half_of(far, h), S_HALF + h, R_HALF + 2 * far + h, across)
     for n, d in enumerate((2, 1, 3)):
         to = slot_of(0, back(d, 4), 0)
         push(qg.at[0], qg.at[to], S_GATHER + 1 + n, R_GATHER + to, at_x(d))
     push(qg.at[0], qg.at[1], S_GATHER + 4, R_GATHER + 1, partner)
-    for dz, dx, dc in GROUP_RELATIVE[1:]:
-        to = slot_of(dz, back(dx, 4), dc)
-        push(
-            meta.at[0],
-            meta.at[to],
-            S_META + slot_of(dz, dx, dc),
-            R_META + to,
-            in_group(dz, dx, dc),
-        )
-
     first_lane = lax.broadcasted_iota(jnp.int32, (128, 128), 1) == 0
     token = lax.broadcasted_iota(jnp.int32, (128, 128), 0)
     for p in range(plen.shape[0]):
@@ -263,24 +277,31 @@
     def relay_x(dz, first):
         for n, d in enumerate((1, 2, 3)):
             here, there = slot_of(dz, d, 0), slot_of(dz, d, 1)
-            arrived(qg.at[here], R_GATHER + here)
+            if dz:
+                for h in range(2):
+                    arrived(half_of(here, h), R_HALF + 2 * here + h)
+            else:
+                arrived(qg.at[here], R_GATHER + here)
             push(qg.at[here], qg.at[there], first + n, R_GATHER + there, partner)
 
     def relay_z():
-        here = slot_of(1, 0, 0)
-        arrived(qg.at[here], R_GATHER + here)
-        for n, d in enumerate((2, 1, 3)):
-            to = slot_of(1, back(d, 4), 0)
-            push(qg.at[here], qg.at[to], S_GATHER + 8 + n, R_GATHER + to, at_x(d))
-        push(qg.at[here], qg.at[here + 1], S_GATHER + 11, R_GATHER + here + 1, partner)
+        for h in range(2):
+            arrived(half_of(far, h), R_HALF + 2 * far + h)
+            for n, d in enumerate((2, 1, 3)):
+                to = slot_of(1, back(d, 4), 0)
+                push(
+                    half_of(far, h),
+                    half_of(to, h),
+                    S_HALF + 2 + 3 * h + n,
+                    R_HALF + 2 * to + h,
+                    at_x(d),
+                )
+        push(qg.at[far], qg.at[far + 1], S_GATHER, R_GATHER + far + 1, partner)
 
     def count_hard():
         for dz, dx, dc in GROUP_RELATIVE:
-            slot = slot_of(dz, dx, dc)
-            if slot:
-                arrived(meta.at[slot], R_META + slot)
             first = pl.multiple_of(group_of(dz, dx, dc) * 8, 8)
-            meta_rows[pl.ds(first, 8), :] = meta[slot]
+            meta_rows[pl.ds(first, 8), :] = qg[slot_of(dz, dx, dc), 256:272].astype(F32)[0:8]
         turned = meta_rows[...].T
         own = (
             group_of(0, 0, 0) * 16 + lax.broadcasted_iota(jnp.int32, (16, 128), 0)
@@ -296,7 +317,7 @@
     height = step * 128
 
     def grow(k):
-        block = jnp.concatenate([qg[k], one_lane[...]], axis=1)
+        block = jnp.concatenate([qg[k, 0:256], one_lane[...]], axis=1)
         for n in range(passages // step):
             similar = contract_last(pe[n * height : (n + 1) * height, :], block)
             grown = jnp.exp2(similar * EXP2_SCALE)
@@ -329,24 +350,27 @@
 
     score_ref[...] = jnp.zeros_like(score_ref)
     grow(0)
+    pl.semaphore_wait(entry.at[0], 3)
+    pl.semaphore_signal(entry.at[1], inc=1, device_id=partner, device_id_type=MESH)
     relay_x(0, S_GATHER + 5)
     arrived(qg.at[1], R_GATHER + 1)
     grow(1)
 
     def forward(t, carry):
-        @pl.when(t == 2)
+        @pl.when(t == 1)
         def _():
             relay_z()
 
-        @pl.when(t == 3)
+        @pl.when(t == 5)
+        def _():
+            relay_x(1, S_GATHER + 8)
+
+        arrived(qg.at[2 * t + 1], R_GATHER + 2 * t + 1)
+
+        @pl.when(t == 7)
         def _():
             count_hard()
 
-        @pl.when(t == 5)
-        def _():
-            relay_x(1, S_GATHER + 12)
-
-        arrived(qg.at[2 * t + 1], R_GATHER + 2 * t + 1)
         score(t - 1)
         grow(2 * t)
         grow(2 * t + 1)
@@ -360,6 +384,7 @@
         lax.broadcasted_iota(jnp.int32, (128, tokens), 1) // 32
         == lax.rem(lax.broadcasted_iota(jnp.int32, (128, tokens), 0), 8)
     ).astype(F32)
+    pl.semaphore_wait(entry.at[1], 1)
     counts, chosen = counts_ref[...], chosen_ref[...]
     grown = jnp.exp(scores - SHIFT)
     hard = counts * grown
@@ -445,9 +470,15 @@
     def backward(j, carry):
         dz = 1 - j // 4
         k = dz * 8 + lax.rem(j + 1, 4) * 2
-        both = qg[pl.ds(k, 2)].reshape(2 * tokens, qg.shape[2])
+        both = qg[pl.ds(k, 2), 0:256].reshape(2 * tokens, qg.shape[2])
         acc = None
         for n in range(passages // BSTEP):
+            if n == 2:
+
+                @pl.when(j >= 1)
+                def _():
+                    combine(j - 1)
+
             parts = []
             for i in range(BSTEP):
                 p = n * BSTEP + i
@@ -468,11 +499,7 @@
         push(qgt.at[2 * j], rc.at[j], S_QC + j, R_QC + j, partner)
         qgt[2 * j + 1] = acc[:, :tokens].astype(BF16)
 
-        @pl.when(j >= 1)
-        def _():
-            combine(j - 1)
-
-        @pl.when(j == 6)
+        @pl.when(j == 5)
         def _():
             zs[...] = over_x(0).astype(BF16)
             push(zs, rz, S_QZ, R_QZ, across)
@@ -480,7 +507,6 @@
         return carry
 
     lax.fori_loop(0, 8, backward, 0)
-    combine(7)
 
     for k in range(P_CHUNKS):
         at = pl.ds(k * rows_in, rows_in)
@@ -490,6 +516,7 @@
     w_t = jnp.dot(pb_t[...], ph[...], preferred_element_type=F32)
     w_loc[...] = w_t.T
 
+    combine(7)
     arrived(rz, R_QZ)
     whole = over_x(1) + rz[...].astype(F32)
     qb = norm_vjp(q_pre[...], whole.T).astype(BF16)
@@ -534,10 +561,11 @@
     for k in range(32):
         total_out[k * piece : (k + 1) * piece, :] = parts[k].astype(F32)
 
-    for n in range(15):
+    for n in range(11):
         sent(qg.at[0], S_GATHER + n)
+    for n in range(8):
+        sent(half_of(0, 0 if n in (0, 2, 3, 4) else 1), S_HALF + n)
     for n in range(1, 16):
-        sent(meta.at[0], S_META + n)
         sent(st_send, S_STATS + n)
     for n in range(1, 32):
         sent(h_recv.at[pl.ds(0, 1)], S_HARD + n)
@@ -581,6 +609,9 @@
     smem = pl.BlockSpec(memory_space=pltpu.SMEM)
     hbm = pl.BlockSpec(memory_space=pl.ANY)
     scratch = [
+        pltpu.SMEM(passage_len.shape, jnp.int32),
+        pltpu.SMEM(positive.shape, jnp.int32),
+        pltpu.VMEM(hard_ids.shape, jnp.int32),
         pltpu.VMEM((q_rows, width), BF16),
         pltpu.VMEM((width, dim), BF16),
         pltpu.VMEM((p_rows, width), BF16),
@@ -589,14 +620,14 @@
         pltpu.VMEM((p_rows, 2 * dim), BF16),
         pltpu.VMEM((dim, p_rows), BF16),
         pltpu.VMEM((width, q_rows), BF16),
-        pltpu.VMEM((16, q_rows, dim), BF16),
+        pltpu.VMEM((16, q_rows + 16, dim), BF16),
         pltpu.VMEM((16, p_rows, q_rows), BF16),
         pltpu.VMEM((16, passages, q_rows), F32),
         pltpu.VMEM((q_rows, 128), F32),
         pltpu.VMEM((q_rows, 128), BF16),
         pltpu.VMEM((16, passages, q_rows), F32),
         pltpu.VMEM((p_rows, dim), F32),
-        pltpu.VMEM((16, 8, 128), F32),
+        pltpu.VMEM((16, 128), F32),
         pltpu.VMEM((128, 128), F32),
         pltpu.VMEM((passages, 128), F32),
         pltpu.VMEM((passages, 128), F32),
@@ -624,6 +655,7 @@
         pltpu.SemaphoreType.DMA((SEND.total,)),
         pltpu.SemaphoreType.DMA((RECV.total,)),
         pltpu.SemaphoreType.DMA((LOCAL.total,)),
+        pltpu.SemaphoreType.REGULAR((2,)),
     ]
     losses, total, query_grad, passage_grad = pl.pallas_call(
         kernel,
@@ -633,7 +665,7 @@
             pltpu.VMEM((q_rows, width), BF16),
             pltpu.VMEM((p_rows, width), BF16),
         ),
-        in_specs=[smem, smem, hbm, hbm, hbm, vmem],
+        in_specs=[hbm] * 6,
         out_specs=(vmem, vmem, vmem, vmem),
         scratch_shapes=scratch,
         compiler_params=pltpu.CompilerParams(

time: 74.7 us -> 72.1 us (0.965)
  Pallas kernels: 74 us -> 71.4 us
    pallas_call x1, Pallas kernels: 71.4 us -> 68.9 us  [local(): pl.pallas_call(kernel, out_shape=(pltpu.VMEM((8, 128), F32), pltpu.VMEM((...]
where the time goes in v5:
time: 72.1 us
  Pallas kernels  71.4 us (99%)
    pallas_call x1, Pallas kernels, local(): pl.pallas_call(kernel, out_shape=(pltpu.VMEM((8, 128), F32), pltpu.VMEM((...  68.9 us
    pallas_call x1, Pallas kernels, local(): pl.pallas_call(write_out, out_shape=(jax.ShapeDtypeStruct((queries,), F32...  2.52 us

profile of v5, /device:TPU:1, one launch (start us, length us, event | category | flops | bytes accessed | tf_op | source)
XLA Modules:
  0.0 72.1 jit_solution(14171800853165478931)
XLA Ops:
  0.6 68.9 %late_interaction_step.1 = (f32[8,128]{1,0:T(8,128)S(1)}, f32[768,128]{1,0:T(8,128)S(1)}, bf16[256,768]{1,0:T(8,128)(2,1)S(1)}, bf16[2048,768]{1,0:T(8,128)(2,1)S(1)}) custom-call(s32[16]{0:T(128)} %plen_hbm.1, s32[8]{0:T(128)} %positive_hbm.1, bf16[256,768]{1,0:T(8,128)(2,1)} %bitcast.5, bf16[2048,768]{1,0:T(8,128)(2,1)} %bitcast.4, ...), custom_call_target="tpu_custom_call" | custom-call | tf_op jit(solution)/shard_map/late_interaction_step/pallas_call | solution.py:660
  69.5 2.5 %write_out.1 = (f32[8]{0:T(128)}, f32[768,128]{1,0:T(8,128)}, bf16[256,768]{1,0:T(8,128)(2,1)}, bf16[2048,768]{1,0:T(8,128)(2,1)}) custom-call(f32[8,128]{1,0:T(8,128)S(1)} %get-tuple-element.12.losses, f32[768,128]{1,0:T(8,128)S(1)} %get-tuple-element.13.total, bf16[256,768]{1,0:T(8,128)(2,1)S(1)} %get-tuple-element.14.gq, ...), custom_call_target="tpu_custom_call" | custom-call | tf_op jit(solution)/shard_map/write_out/pallas_call | solution.py:683

commit v6 on v5

--- a/solution.py
+++ b/solution.py
@@ -284,19 +284,19 @@
                 arrived(qg.at[here], R_GATHER + here)
             push(qg.at[here], qg.at[there], first + n, R_GATHER + there, partner)
 
-    def relay_z():
-        for h in range(2):
-            arrived(half_of(far, h), R_HALF + 2 * far + h)
-            for n, d in enumerate((2, 1, 3)):
-                to = slot_of(1, back(d, 4), 0)
-                push(
-                    half_of(far, h),
-                    half_of(to, h),
-                    S_HALF + 2 + 3 * h + n,
-                    R_HALF + 2 * to + h,
-                    at_x(d),
-                )
-        push(qg.at[far], qg.at[far + 1], S_GATHER, R_GATHER + far + 1, partner)
+    def relay_z(h):
+        arrived(half_of(far, h), R_HALF + 2 * far + h)
+        for n, d in enumerate((2, 1, 3)):
+            to = slot_of(1, back(d, 4), 0)
+            push(
+                half_of(far, h),
+                half_of(to, h),
+                S_HALF + 2 + 3 * h + n,
+                R_HALF + 2 * to + h,
+                at_x(d),
+            )
+        if h:
+            push(qg.at[far], qg.at[far + 1], S_GATHER, R_GATHER + far + 1, partner)
 
     def count_hard():
         for dz, dx, dc in GROUP_RELATIVE:
@@ -359,7 +359,11 @@
     def forward(t, carry):
         @pl.when(t == 1)
         def _():
-            relay_z()
+            relay_z(0)
+
+        @pl.when(t == 2)
+        def _():
+            relay_z(1)
 
         @pl.when(t == 5)
         def _():
@@ -473,12 +477,6 @@
         both = qg[pl.ds(k, 2), 0:256].reshape(2 * tokens, qg.shape[2])
         acc = None
         for n in range(passages // BSTEP):
-            if n == 2:
-
-                @pl.when(j >= 1)
-                def _():
-                    combine(j - 1)
-
             parts = []
             for i in range(BSTEP):
                 p = n * BSTEP + i
@@ -498,6 +496,10 @@
         qgt[2 * j] = acc[:, tokens:].astype(BF16)
         push(qgt.at[2 * j], rc.at[j], S_QC + j, R_QC + j, partner)
         qgt[2 * j + 1] = acc[:, :tokens].astype(BF16)
+
+        @pl.when(j >= 1)
+        def _():
+            combine(j - 1)
 
         @pl.when(j == 5)
         def _():

time: 72.1 us -> 72.1 us (level)
  no operation moved by 1% of the time
where the time goes in v6:
time: 72.1 us; the launch traced here: 72 us
  Pallas kernels  71.4 us (99%)
    pallas_call x1, Pallas kernels, local(): pl.pallas_call(kernel, out_shape=(pltpu.VMEM((8, 128), F32), pltpu.VMEM((...  68.8 us
    pallas_call x1, Pallas kernels, local(): pl.pallas_call(write_out, out_shape=(jax.ShapeDtypeStruct((queries,), F32...  2.52 us

profile of v6, /device:TPU:1, one launch (start us, length us, event | category | flops | bytes accessed | tf_op | source)
XLA Modules:
  0.0 72.0 jit_solution(7404483945671307015)
XLA Ops:
  0.6 68.8 %late_interaction_step.1 = (f32[8,128]{1,0:T(8,128)S(1)}, f32[768,128]{1,0:T(8,128)S(1)}, bf16[256,768]{1,0:T(8,128)(2,1)S(1)}, bf16[2048,768]{1,0:T(8,128)(2,1)S(1)}) custom-call(s32[16]{0:T(128)} %plen_hbm.1, s32[8]{0:T(128)} %positive_hbm.1, bf16[256,768]{1,0:T(8,128)(2,1)} %bitcast.5, bf16[2048,768]{1,0:T(8,128)(2,1)} %bitcast.4, ...), custom_call_target="tpu_custom_call" | custom-call | tf_op jit(solution)/shard_map/late_interaction_step/pallas_call | solution.py:662
  69.5 2.5 %write_out.1 = (f32[8]{0:T(128)}, f32[768,128]{1,0:T(8,128)}, bf16[256,768]{1,0:T(8,128)(2,1)}, bf16[2048,768]{1,0:T(8,128)(2,1)}) custom-call(f32[8,128]{1,0:T(8,128)S(1)} %get-tuple-element.12.losses, f32[768,128]{1,0:T(8,128)S(1)} %get-tuple-element.13.total, bf16[256,768]{1,0:T(8,128)(2,1)S(1)} %get-tuple-element.14.gq, ...), custom_call_target="tpu_custom_call" | custom-call | tf_op jit(solution)/shard_map/write_out/pallas_call | solution.py:685
